TPU v7x, 32 devices: a whole 2x2x4 slice. The times are simulated.
32 devices in a mesh: dp: 8 (over y, x, core), tensor: 4 (over z).
Axes of the slice: x: 2, y: 2, z: 4, core: 2. Of those that a mesh axis runs over, the one named last changes fastest.
Arguments:
- tokens: bfloat16 [8, 736, 1152], P('dp', 'tensor'), may hold values from -45 to 45
- key_mask: int32 [8, 736], P('dp'), may hold values from 0 to 1, as said below
- query_weight: bfloat16 [1152, 1152], P('dp', 'tensor'), may hold values from -0.1875 to 0.1875
- key_weight: bfloat16 [1152, 1152], P('dp', 'tensor'), may hold values from -0.1875 to 0.1875
- value_weight: bfloat16 [1152, 1152], P('dp', 'tensor'), may hold values from -0.1875 to 0.1875
- out_weight: bfloat16 [1152, 1152], P('tensor', 'dp'), may hold values from -0.375 to 0.375
- up_weight: bfloat16 [1152, 4304], P('dp', 'tensor'), may hold values from -0.1875 to 0.1875
- down_weight: bfloat16 [4304, 1152], P('tensor', 'dp'), may hold values from -0.09375 to 0.09375
- first_gain: bfloat16 [1152], P('dp'), may hold values from 0.5 to 1.5
- first_shift: bfloat16 [1152], P('dp'), may hold values from -3 to 3
- query_bias: bfloat16 [1152], P('dp'), may hold values from -3 to 3
- value_bias: bfloat16 [1152], P('dp'), may hold values from -3 to 3
- out_bias: bfloat16 [1152], P('dp'), may hold values from -3 to 3
- second_gain: bfloat16 [1152], P('dp'), may hold values from 0.5 to 1.5
- second_shift: bfloat16 [1152], P('dp'), may hold values from -3 to 3
- up_bias: bfloat16 [4304], P('dp'), may hold values from -3 to 3
- down_bias: bfloat16 [1152], P('dp'), may hold values from -3 to 3
- cotangent: bfloat16 [8, 736, 1152], P('dp', 'tensor'), may hold values from -6 to 6
Outputs:
- output: bfloat16 [8, 736, 1152], P('dp', 'tensor')
- input_grad: float32 [8, 736, 1152], P('dp', 'tensor')
- query_grad: float32 [1152, 1152], P('dp', 'tensor')
- key_grad: float32 [1152, 1152], P('dp', 'tensor')
- value_grad: float32 [1152, 1152], P('dp', 'tensor')
- out_grad: float32 [1152, 1152], P('tensor', 'dp')
- up_grad: float32 [1152, 4304], P('dp', 'tensor')
- down_grad: float32 [4304, 1152], P('tensor', 'dp')
- first_gain_grad: float32 [1152], P('dp')
- first_shift_grad: float32 [1152], P('dp')
- query_bias_grad: float32 [1152], P('dp')
- value_bias_grad: float32 [1152], P('dp')
- out_bias_grad: float32 [1152], P('dp')
- second_gain_grad: float32 [1152], P('dp')
- second_shift_grad: float32 [1152], P('dp')
- up_bias_grad: float32 [4304], P('dp')
- down_bias_grad: float32 [1152], P('dp')
Inputs may be any that keep to these rules, and one draw needn't show every extreme that they name: `key_mask`: each image's ones form a prefix of its positions, at least its first three quarters.
All inputs are finite; a program needn't handle non-finite values.
Results may differ from a plain program's by a relative error of at most 0.017.
The roundings to bfloat16 on the way count: a program that leaves them out, or rounds other values in their place, can miss the bound.
Values may be sent and summed in bfloat16 or wider, within the bound.
A program may use at most 128 MiB of HBM per device.

v0:
```python
from functools import partial
import math

import jax
import jax.numpy as jnp
from jax import lax
from jax.sharding import PartitionSpec as P

HD = 72


EPSILON = 1e-06
GELU_COEF = 0.7978845608028654
MASK_FILL = -1e30


def norm_forward(inputs, gain_vec, shift_vec):
    centred = inputs - jnp.mean(inputs, axis=-1, keepdims=True)
    inv_std = lax.rsqrt(jnp.mean(centred * centred, axis=-1, keepdims=True) + EPSILON)
    normed = centred * inv_std
    return (normed * gain_vec + shift_vec, normed, inv_std)


def norm_backward(grad_in, normed, inv_std, gain_vec):
    scaled = grad_in * gain_vec
    return inv_std * (
        scaled
        - jnp.mean(scaled, axis=-1, keepdims=True)
        - normed * jnp.mean(scaled * normed, axis=-1, keepdims=True)
    )


def gelu_pair(pre_act):
    tanh_val = jnp.tanh(GELU_COEF * (pre_act + 0.044715 * pre_act * pre_act * pre_act))
    gelu_value = 0.5 * pre_act * (1.0 + tanh_val)
    gelu_slope = 0.5 * (1.0 + tanh_val) + 0.5 * pre_act * (
        1.0 - tanh_val * tanh_val
    ) * GELU_COEF * (1.0 + 3.0 * 0.044715 * pre_act * pre_act)
    return (gelu_value, gelu_slope)


def mat_dot(left, right):
    return jnp.dot(left, right, preferred_element_type=jnp.float32)


def gather_rows(local):
    return lax.all_gather(local, "tensor", axis=1, tiled=True)


def sum_rows(partial_term):
    return lax.psum_scatter(
        partial_term.astype(jnp.bfloat16), "tensor", scatter_dimension=1, tiled=True
    ).astype(jnp.float32)


def attend_image(packed):
    query_img, keys_img, values_img, valid_img = packed
    scores = jnp.einsum("qhd,khd->hqk", query_img, keys_img, preferred_element_type=jnp.float32)
    scores = jnp.where(valid_img[None, None, :] > 0, scores, MASK_FILL)
    highest = jnp.max(scores, axis=-1, keepdims=True)
    logsum = highest + jnp.log(jnp.sum(jnp.exp(scores - highest), axis=-1, keepdims=True))
    probs = jnp.exp(scores - logsum).astype(jnp.bfloat16)
    mixed = jnp.einsum("hqk,khd->qhd", probs, values_img, preferred_element_type=jnp.float32)
    return (mixed.astype(jnp.bfloat16), logsum[..., 0])


def attend_back(scale_factor, packed):
    query_img, keys_img, values_img, valid_img, logsum_img, mixed_img, grad_img = packed
    scores = jnp.einsum("qhd,khd->hqk", query_img, keys_img, preferred_element_type=jnp.float32)
    scores = jnp.where(valid_img[None, None, :] > 0, scores, MASK_FILL)
    probs_full = jnp.exp(scores - logsum_img[:, :, None])
    probs = probs_full.astype(jnp.bfloat16)
    grad_values = jnp.einsum("hqk,qhd->khd", probs, grad_img, preferred_element_type=jnp.float32)
    grad_probs = jnp.einsum(
        "qhd,khd->hqk", grad_img, values_img, preferred_element_type=jnp.float32
    )
    delta = jnp.sum(grad_img.astype(jnp.float32) * mixed_img.astype(jnp.float32), axis=-1).T
    grad_scores = (probs_full * (grad_probs - delta[:, :, None])).astype(jnp.bfloat16)
    grad_query = (
        jnp.einsum("hqk,khd->qhd", grad_scores, keys_img, preferred_element_type=jnp.float32)
        * scale_factor
    )
    grad_keys = jnp.einsum(
        "hqk,qhd->khd", grad_scores, query_img, preferred_element_type=jnp.float32
    )
    return (grad_query, grad_keys, grad_values)


def vector_share(full_vec, parts, index):
    piece = full_vec.shape[0] // parts
    return lax.dynamic_slice_in_dim(full_vec, index * piece, piece)


def shards(
    tokens,
    key_mask,
    query_weight,
    key_weight,
    value_weight,
    out_weight,
    up_weight,
    down_weight,
    first_gain,
    first_shift,
    query_bias,
    value_bias,
    out_bias,
    second_gain,
    second_shift,
    up_bias,
    down_bias,
    cotangent,
):
    dp_count = lax.axis_size("dp")
    dp_index = lax.axis_index("dp")
    tensor_index = lax.axis_index("tensor")
    images = tokens.shape[0]
    width = tokens.shape[2]
    fetched = (
        lax.all_gather(query_weight, "dp", axis=0, tiled=True),
        lax.all_gather(key_weight, "dp", axis=0, tiled=True),
        lax.all_gather(value_weight, "dp", axis=0, tiled=True),
        lax.all_gather(out_weight, "dp", axis=1, tiled=True),
        lax.all_gather(up_weight, "dp", axis=0, tiled=True),
        lax.all_gather(down_weight, "dp", axis=1, tiled=True),
        lax.all_gather(first_gain, "dp", axis=0, tiled=True),
        lax.all_gather(first_shift, "dp", axis=0, tiled=True),
        lax.all_gather(query_bias, "dp", axis=0, tiled=True),
        lax.all_gather(value_bias, "dp", axis=0, tiled=True),
        lax.all_gather(out_bias, "dp", axis=0, tiled=True),
        lax.all_gather(second_gain, "dp", axis=0, tiled=True),
        lax.all_gather(second_shift, "dp", axis=0, tiled=True),
        lax.all_gather(up_bias, "dp", axis=0, tiled=True),
        lax.all_gather(down_bias, "dp", axis=0, tiled=True),
    )
    query_full, key_full, value_full, out_full, up_full, down_full = fetched[:6]
    (
        gain_one,
        shift_one,
        query_bias_all,
        value_bias_all,
        out_bias_all,
        gain_two,
        shift_two,
        up_bias_all,
        down_bias_all,
    ) = [member.astype(jnp.float32) for member in fetched[6:]]
    head_cols = query_full.shape[1]
    hidden_cols = up_full.shape[1]
    heads_local = head_cols // HD
    query_bias_local = lax.dynamic_slice_in_dim(query_bias_all, tensor_index * head_cols, head_cols)
    value_bias_local = lax.dynamic_slice_in_dim(value_bias_all, tensor_index * head_cols, head_cols)
    up_bias_local = lax.dynamic_slice_in_dim(up_bias_all, tensor_index * hidden_cols, hidden_cols)
    scale_factor = 1.0 / math.sqrt(HD)
    inputs = tokens.astype(jnp.float32)
    first, normed_one, inv_one = norm_forward(inputs, gain_one, shift_one)
    first_rows = gather_rows(first.astype(jnp.bfloat16))
    seq_full = first_rows.shape[1]
    row_shape = (images, seq_full, width)
    head_shape = (images, seq_full, heads_local, HD)
    first_flat = first_rows.reshape(-1, width)
    query = (
        ((mat_dot(first_flat, query_full) + query_bias_local) * scale_factor)
        .astype(jnp.bfloat16)
        .reshape(head_shape)
    )
    keys = mat_dot(first_flat, key_full).astype(jnp.bfloat16).reshape(head_shape)
    values = (
        (mat_dot(first_flat, value_full) + value_bias_local)
        .astype(jnp.bfloat16)
        .reshape(head_shape)
    )
    mixed, logsum = lax.map(attend_image, (query, keys, values, key_mask))
    mixed_flat = mixed.reshape(-1, head_cols)
    hidden = inputs + sum_rows(mat_dot(mixed_flat, out_full).reshape(row_shape)) + out_bias_all
    second, normed_two, inv_two = norm_forward(hidden, gain_two, shift_two)
    second_flat = gather_rows(second.astype(jnp.bfloat16)).reshape(-1, width)
    pre_act = mat_dot(second_flat, up_full) + up_bias_local
    gelu_value, gelu_slope = gelu_pair(pre_act)
    act = gelu_value.astype(jnp.bfloat16)
    output = (hidden + sum_rows(mat_dot(act, down_full).reshape(row_shape)) + down_bias_all).astype(
        jnp.bfloat16
    )
    query_back, key_back, value_back, out_back, up_back, down_back = (
        lax.all_gather(query_weight, "dp", axis=0, tiled=True),
        lax.all_gather(key_weight, "dp", axis=0, tiled=True),
        lax.all_gather(value_weight, "dp", axis=0, tiled=True),
        lax.all_gather(out_weight, "dp", axis=1, tiled=True),
        lax.all_gather(up_weight, "dp", axis=0, tiled=True),
        lax.all_gather(down_weight, "dp", axis=1, tiled=True),
    )
    grad_out = cotangent.astype(jnp.float32)
    down_bias_grad = jnp.sum(grad_out, axis=(0, 1))
    grad_rows = gather_rows(cotangent).reshape(-1, width)
    down_grad = mat_dot(act.T, grad_rows)
    grad_pre = mat_dot(grad_rows, down_back.T) * gelu_slope
    up_bias_part = jnp.sum(grad_pre, axis=0)
    grad_pre_low = grad_pre.astype(jnp.bfloat16)
    up_grad = mat_dot(second_flat.T, grad_pre_low)
    grad_second = sum_rows(mat_dot(grad_pre_low, up_back.T).reshape(row_shape))
    second_gain_grad = jnp.sum(grad_second * normed_two, axis=(0, 1))
    second_shift_grad = jnp.sum(grad_second, axis=(0, 1))
    grad_hidden = grad_out + norm_backward(grad_second, normed_two, inv_two, gain_two)
    out_bias_grad = jnp.sum(grad_hidden, axis=(0, 1))
    hidden_rows = gather_rows(grad_hidden.astype(jnp.bfloat16)).reshape(-1, width)
    grad_mixed = mat_dot(hidden_rows, out_back.T).astype(jnp.bfloat16)
    out_grad = mat_dot(mixed_flat.T, hidden_rows)
    grad_query_f, grad_keys_f, grad_values_f = lax.map(
        partial(attend_back, scale_factor),
        (query, keys, values, key_mask, logsum, mixed, grad_mixed.reshape(head_shape)),
    )
    grad_query_f = grad_query_f.reshape(-1, head_cols)
    grad_keys_f = grad_keys_f.reshape(-1, head_cols)
    grad_values_f = grad_values_f.reshape(-1, head_cols)
    query_bias_part = jnp.sum(grad_query_f, axis=0)
    value_bias_part = jnp.sum(grad_values_f, axis=0)
    grad_query = grad_query_f.astype(jnp.bfloat16)
    grad_keys = grad_keys_f.astype(jnp.bfloat16)
    grad_values = grad_values_f.astype(jnp.bfloat16)
    query_grad = mat_dot(first_flat.T, grad_query)
    key_grad = mat_dot(first_flat.T, grad_keys)
    value_grad = mat_dot(first_flat.T, grad_values)
    first_term = (
        mat_dot(grad_query, query_back.T)
        + mat_dot(grad_keys, key_back.T)
        + mat_dot(grad_values, value_back.T)
    )
    grad_first = sum_rows(first_term.reshape(row_shape))
    first_gain_grad = jnp.sum(grad_first * normed_one, axis=(0, 1))
    first_shift_grad = jnp.sum(grad_first, axis=(0, 1))
    input_grad = grad_hidden + norm_backward(grad_first, normed_one, inv_one, gain_one)
    matrix_shares = (
        lax.psum_scatter(query_grad, "dp", scatter_dimension=0, tiled=True),
        lax.psum_scatter(key_grad, "dp", scatter_dimension=0, tiled=True),
        lax.psum_scatter(value_grad, "dp", scatter_dimension=0, tiled=True),
        lax.psum_scatter(out_grad, "dp", scatter_dimension=1, tiled=True),
        lax.psum_scatter(up_grad, "dp", scatter_dimension=0, tiled=True),
        lax.psum_scatter(down_grad, "dp", scatter_dimension=1, tiled=True),
    )
    query_bias_full = lax.dynamic_update_slice_in_dim(
        jnp.zeros((width,), jnp.float32), query_bias_part, tensor_index * head_cols, 0
    )
    value_bias_full = lax.dynamic_update_slice_in_dim(
        jnp.zeros((width,), jnp.float32), value_bias_part, tensor_index * head_cols, 0
    )
    up_bias_full = lax.dynamic_update_slice_in_dim(
        jnp.zeros((up_bias_all.shape[0],), jnp.float32), up_bias_part, tensor_index * hidden_cols, 0
    )
    vector_sums = lax.psum(
        (
            first_gain_grad,
            first_shift_grad,
            query_bias_full,
            value_bias_full,
            out_bias_grad,
            second_gain_grad,
            second_shift_grad,
            up_bias_full,
            down_bias_grad,
        ),
        ("dp", "tensor"),
    )
    vector_parts = tuple((vector_share(member, dp_count, dp_index) for member in vector_sums))
    return (output, input_grad) + tuple(matrix_shares) + vector_parts


def solution(mesh):
    return jax.shard_map(
        shards,
        mesh=mesh,
        in_specs=(
            P("dp", "tensor", None),
            P("dp", None),
            P("dp", "tensor"),
            P("dp", "tensor"),
            P("dp", "tensor"),
            P("tensor", "dp"),
            P("dp", "tensor"),
            P("tensor", "dp"),
            P("dp"),
            P("dp"),
            P("dp"),
            P("dp"),
            P("dp"),
            P("dp"),
            P("dp"),
            P("dp"),
            P("dp"),
            P("dp", "tensor", None),
        ),
        out_specs=(
            P("dp", "tensor", None),
            P("dp", "tensor", None),
            P("dp", "tensor"),
            P("dp", "tensor"),
            P("dp", "tensor"),
            P("tensor", "dp"),
            P("dp", "tensor"),
            P("tensor", "dp"),
            P("dp"),
            P("dp"),
            P("dp"),
            P("dp"),
            P("dp"),
            P("dp"),
            P("dp"),
            P("dp"),
            P("dp"),
        ),
        check_vma=False,
    )
```

profile of v0, /device:TPU:0, one launch (start us, length us, event | category | flops | bytes accessed | tf_op | source)
XLA Modules:
  0.0 748.9 jit_solution(14068338893583376241)
XLA Ops:
  8.1 1.3 dynamic-slice.1
  10.7 1.1 convert_reduce_fusion.2
  11.9 1.3 fusion.70
  13.2 0.9 dynamic-update-slice.3
  14.0 0.8 dynamic-update-slice.2
  14.9 0.8 dynamic-update-slice
  15.7 0.8 dynamic-update-slice.1
  16.6 0.8 dynamic-update-slice.4
  19.9 0.9 dynamic-update-slice.7
  20.8 26.1 %all-reduce.14 = (bf16[1152]{0:T(1024)(128)(2,1)S(1)}, bf16[1152]{0:T(1024)(128)(2,1)S(1)}, bf16[1152]{0:T(1024)(128)(2,1)S(1)}, bf16[1152]{0:T(1024)(128)(2,1)S...) all-reduce(bf16[1152]{0:T(1024)(128)(2,1)S(1)} %dynamic-update-slic, ...), channel_id=1, replica_groups=mesh['dp'=8,'tensor'=4] {'dp'}, use_global_device_ids=true, to_apply=%add.6 | all-reduce | flops 13520 | bytes 54080
  46.9 2.0 fusion.66
  49.9 10.0 %all_gather.68 = bf16[1152,288]{1,0:T(8,128)(2,1)S(1)} all-gather(bf16[144,288]{1,0:T(8,128)(2,1)} %param.20), channel_id=1, replica_groups=mesh['dp'=8,'tensor'=4] {'dp'}, dimensions={0}, use_global_device_ids=true | all-gather | bytes 746496 | tf_op jit(solution)/shard_map/all_gather | solution.py:120
  59.9 10.5 %all_gather.70 = bf16[1152,288]{1,0:T(8,128)(2,1)S(1)} all-gather(bf16[144,288]{1,0:T(8,128)(2,1)S(1)} %copy-done.18), channel_id=1, replica_groups=mesh['dp'=8,'tensor'=4] {'dp'}, dimensions={0}, use_global_device_ids=true | all-gather | bytes 746496 | tf_op jit(solution)/shard_map/all_gather | solution.py:121
  70.4 10.2 %all_gather.66 = bf16[1152,288]{1,0:T(8,128)(2,1)S(1)} all-gather(bf16[144,288]{1,0:T(8,128)(2,1)S(1)} %copy-done.19), channel_id=1, replica_groups=mesh['dp'=8,'tensor'=4] {'dp'}, dimensions={0}, use_global_device_ids=true | all-gather | bytes 746496 | tf_op jit(solution)/shard_map/all_gather | solution.py:122
  80.5 11.8 %all_gather.71 = bf16[288,1152]{0,1:T(8,128)(2,1)} all-gather(bf16[288,144]{0,1:T(8,128)(2,1)S(1)} %copy-done.20), channel_id=1, replica_groups=mesh['dp'=8,'tensor'=4] {'dp'}, dimensions={1}, use_global_device_ids=true | all-gather | bytes 746496 | tf_op jit(solution)/shard_map/all_gather | solution.py:123
  92.3 2.4 fusion.49
  95.6 1.7 select_reduce_fusion
  97.3 1.8 exponential_reduce_fusion
  100.7 1.9 convolution_convert_fusion.4
  103.4 2.4 fusion.10
  106.5 37.1 %reduce-scatter.35.cloned.1.call-done = bf16[1,184,1152]{2,1,0:T(8,128)(2,1)} async-done(((bf16[1,736,1152]{2,1,0:T(8,128)(2,1)}), bf16[1,184,1152]{2,1,0:T(8,128)(2,1)}) %reduce-scatter.35.cloned.1.call-update) | async-done | bytes 423952
  143.6 1.2 fusion.80
  144.8 1.3 multiply_reduce_fusion.1
  146.1 2.0 add_convert_fusion.1
  149.8 36.8 %all-gather.9.cloned.1.call-done = bf16[1,736,1152]{2,1,0:T(8,128)(2,1)} async-done(((bf16[1,184,1152]{2,1,0:T(8,128)(2,1)}), bf16[1,736,1152]{2,1,0:T(8,128)(2,1)}) %all-gather.9.cloned.1.call-update) | async-done | bytes 1695760 | tf_op jit(solution)/shard_map/all_gather | solution.py:47
  186.6 6.4 convolution_add_fusion.2
  193.1 32.8 %all-gather.15.cloned.1.call-done = bf16[1,736,1152]{2,1,0:T(8,128)(2,1)} async-done(((bf16[1,184,1152]{2,1,0:T(8,128)(2,1)}), bf16[1,736,1152]{2,1,0:T(8,128)(2,1)}) %all-gather.15.cloned.1.call-update) | async-done | bytes 1695760 | tf_op jit(solution)/shard_map/all_gather | solution.py:47
  225.9 30.9 %all-gather.13.cloned.1.call-done = bf16[1076,1152]{0,1:T(8,128)(2,1)} async-done(((bf16[1076,144]{0,1:T(8,128)(2,1)}), bf16[1076,1152]{0,1:T(8,128)(2,1)}) %all-gather.13.cloned.1.call-update) | async-done | bytes 2479120 | tf_op jit(solution)/shard_map/all_gather | solution.py:125
  256.8 8.2 %fusion.86 = (f32[1076]{0:T(1024)}, bf16[736,1076]{0,1:T(8,128)(2,1)S(1)}) fusion(f32[736,1076]{0,1:T(8,128)} %convolution_add_fusion.2, bf16[1076,1152]{0,1:T(8,128)(2,1)} %all-gather.13.cloned.1.call-done, bf16[1,736,1152]{2,1,0:T(8,128)(2,1)} %all-gather.15.cloned.1.call-done), kind=kOutput, calls=%fused_computation.117 | convolution fusion | flops 1840458240 | bytes 8930768 | tf_op jit(solution)/shard_map/dot_general | solution.py:43
  265.0 1.2 copy-done.29
  266.2 4.0 fusion.8
  270.2 7.2 fusion.7
  277.5 30.1 %reduce-scatter.39.cloned.1.call-done = bf16[1,184,1152]{2,1,0:T(8,128)(2,1)} async-done(((bf16[1,736,1152]{2,1,0:T(8,128)(2,1)}), bf16[1,184,1152]{2,1,0:T(8,128)(2,1)}) %reduce-scatter.39.cloned.1.call-update) | async-done | bytes 423952
  307.6 1.6 fusion.76
  309.8 36.8 %reduce-scatter.37.cloned.1.call-done = bf16[1,184,1152]{2,1,0:T(8,128)(2,1)} async-done(((bf16[1,736,1152]{2,1,0:T(8,128)(2,1)}), bf16[1,184,1152]{2,1,0:T(8,128)(2,1)}) %reduce-scatter.37.cloned.1.call-update) | async-done | bytes 423952
  346.6 2.7 fusion.83
  350.5 38.2 %all-gather.17.cloned.1.call-done = bf16[1,736,1152]{2,1,0:T(8,128)(2,1)} async-done(((bf16[1,184,1152]{2,1,0:T(8,128)(2,1)}), bf16[1,736,1152]{2,1,0:T(8,128)(2,1)}) %all-gather.17.cloned.1.call-update) | async-done | bytes 1695760 | tf_op jit(solution)/shard_map/all_gather | solution.py:47
  388.8 2.5 fusion.52
  391.2 1.2 multiply_reduce_fusion
  392.4 5.6 fusion.84
  398.1 5.6 multiply_convert_fusion
  403.7 1.4 convolution_convert_fusion.3
  405.2 1.0 fusion.85
  406.2 1.1 fusion.87
  407.5 1.2 convolution_add_fusion.1
  408.7 2.4 fusion.9
  411.1 7.4 fusion.15
  418.8 1.2 copy-done.26
  420.0 6.5 fusion.18
  426.5 0.9 copy-done.17
  427.4 3.9 fusion.11
  431.5 3.9 fusion.21
  435.5 3.9 fusion.25
  439.5 3.8 fusion.23
  444.3 2.7 reduce-scatter.41.cloned.1.call-done
  447.0 1.5 fusion.77
  448.5 41.8 %all-reduce.13 = (f32[1152]{0:T(1024)S(1)}, f32[1152]{0:T(1024)S(1)}, f32[1152]{0:T(1024)S(1)}, f32[1152]{0:T(1024)S(1)}, f32[1152]{0:T(1024)S(1)}, /*index=5*/f...) all-reduce(f32[1152]{0:T(1024)S(1)} %get-tuple-element.73, ...), channel_id=1, replica_groups=mesh['dp'=8,'tensor'=4] {'dp','tensor'}, use_global_device_ids=true, to_apply=%region_22.23 | all-reduce | flops 13520 | bytes 108160 | tf_op jit(solution)/shard_map/psum | solution.py:249
  496.1 2.2 fusion.69
  498.3 9.4 %reduce-scatter.33.cloned.1.call-done = f32[1076,144]{0,1:T(8,128)} async-done(((f32[1076,1152]{0,1:T(8,128)}), f32[1076,144]{0,1:T(8,128)}) %reduce-scatter.33.cloned.1.call-update) | async-done | bytes 619792 | tf_op jit(solution)/shard_map/reduce_scatter | solution.py:238
  507.7 61.1 %reduce-scatter.31.cloned.1.call-done = f32[144,1076]{1,0:T(8,128)} async-done(((f32[1152,1076]{1,0:T(8,128)}), f32[144,1076]{1,0:T(8,128)}) %reduce-scatter.31.cloned.1.call-update) | async-done | bytes 619792 | tf_op jit(solution)/shard_map/reduce_scatter | solution.py:237
  568.8 43.1 %reduce-scatter.29.cloned.1.call-done = f32[288,144]{0,1:T(8,128)} async-done(((f32[288,1152]{0,1:T(8,128)}), f32[288,144]{0,1:T(8,128)}) %reduce-scatter.29.cloned.1.call-update) | async-done | bytes 165904 | tf_op jit(solution)/shard_map/reduce_scatter | solution.py:236
  611.9 43.1 %reduce-scatter.27.cloned.1.call-done = f32[144,288]{1,0:T(8,128)} async-done(((f32[1152,288]{1,0:T(8,128)}), f32[144,288]{1,0:T(8,128)}) %reduce-scatter.27.cloned.1.call-update) | async-done | bytes 165904 | tf_op jit(solution)/shard_map/reduce_scatter | solution.py:235
  655.0 43.2 %reduce-scatter.23.cloned.1.call-done = f32[144,288]{1,0:T(8,128)} async-done(((f32[1152,288]{1,0:T(8,128)}), f32[144,288]{1,0:T(8,128)}) %reduce-scatter.23.cloned.1.call-update) | async-done | bytes 165904 | tf_op jit(solution)/shard_map/reduce_scatter | solution.py:233
  698.3 43.1 %reduce-scatter.25.cloned.1.call-done = f32[144,288]{1,0:T(8,128)} async-done(((f32[1152,288]{1,0:T(8,128)}), f32[144,288]{1,0:T(8,128)}) %reduce-scatter.25.cloned.1.call-update) | async-done | bytes 165904 | tf_op jit(solution)/shard_map/reduce_scatter | solution.py:234
  (141 shorter events, 18.5 us)
Async XLA Ops:
  8.0 51.8 %copy-start.18 = (bf16[144,288]{1,0:T(8,128)(2,1)S(1)}, bf16[144,288]{1,0:T(8,128)(2,1)}, u32[]{:S(2)}) copy-start(bf16[144,288]{1,0:T(8,128)(2,1)} %param.21) | copy-start | bytes 248836
  8.0 62.3 %copy-start.19 = (bf16[144,288]{1,0:T(8,128)(2,1)S(1)}, bf16[144,288]{1,0:T(8,128)(2,1)}, u32[]{:S(2)}) copy-start(bf16[144,288]{1,0:T(8,128)(2,1)} %param.22) | copy-start | bytes 248836
  8.0 72.5 %copy-start.20 = (bf16[288,144]{0,1:T(8,128)(2,1)S(1)}, bf16[288,144]{0,1:T(8,128)(2,1)}, u32[]{:S(2)}) copy-start(bf16[288,144]{0,1:T(8,128)(2,1)} %param.23) | copy-start | bytes 248836
  8.1 84.3 %all-gather.7.cloned.1.call-start = ((), (), s32[]{:S(2)}) async-start(), calls=%async_computation.10 | async-start | bytes 2119680 | tf_op jit(solution)/shard_map/all_gather | solution.py:47
  48.9 94.6 %reduce-scatter.35.cloned.1.call-start = ((), (), s32[]{:S(2)}) async-start(), calls=%async_computation.22 | async-start | bytes 2119680
  70.4 25.2 %copy-start.3 = (bf16[1152,288]{1,0:T(8,128)(2,1)}, bf16[1152,288]{1,0:T(8,128)(2,1)S(1)}, u32[]{:S(2)}) copy-start(bf16[1152,288]{1,0:T(8,128)(2,1)S(1)} %all_gather.70) | copy-start | bytes 1990660
  92.3 2.4 copy-start.25
  94.7 2.6 copy-start.7
  95.5 1.7 copy-start.9
  97.3 3.4 copy-start.1
  99.1 3.5 copy-start.21
  99.9 2.7 copy-start.27
  100.7 2.6 copy-start.13
  102.6 0.8 copy-start.16
  102.6 40.9 %copy-start = (bf16[1,184,1152]{2,1,0:T(8,128)(2,1)S(1)}, bf16[1,184,1152]{2,1,0:T(8,128)(2,1)}, u32[]{:S(2)}) copy-start(bf16[1,184,1152]{2,1,0:T(8,128)(2,1)} %param.18) | copy-start | bytes 1271812
  105.8 44.0 %all-gather.11.cloned.1.call-start = ((), (), s32[]{:S(2)}) async-start(), calls=%async_computation.12 | async-start | bytes 2985984 | tf_op jit(solution)/shard_map/all_gather | solution.py:124
  106.4 80.2 %all-gather.9.cloned.1.call-start = ((), (), s32[]{:S(2)}) async-start(), calls=%async_computation.11 | async-start | bytes 2119680 | tf_op jit(solution)/shard_map/all_gather | solution.py:47
  148.2 77.7 %all-gather.15.cloned.1.call-start = ((), (), s32[]{:S(2)}) async-start(), calls=%async_computation.14 | async-start | bytes 2119680 | tf_op jit(solution)/shard_map/all_gather | solution.py:47
  148.7 108.0 %all-gather.13.cloned.1.call-start = ((), (), s32[]{:S(2)}) async-start(), calls=%async_computation.13 | async-start | bytes 2985984 | tf_op jit(solution)/shard_map/all_gather | solution.py:125
  149.5 158.2 %reduce-scatter.39.cloned.1.call-start = ((), (), s32[]{:S(2)}) async-start(), calls=%async_computation.24 | async-start | bytes 2119680
  256.8 9.4 %copy-start.24 = (bf16[1152,1076]{1,0:T(8,128)(2,1)S(1)}, bf16[1152,1076]{1,0:T(8,128)(2,1)}, u32[]{:S(2)}) copy-start(bf16[1152,1076]{1,0:T(8,128)(2,1)} %all-gather.11.cloned.1.call-done) | copy-start | bytes 7437316
  265.0 1.2 copy-start.29
  270.2 37.5 %copy-start.2 = (bf16[1,184,1152]{2,1,0:T(8,128)(2,1)S(1)}, bf16[1,184,1152]{2,1,0:T(8,128)(2,1)}, u32[]{:S(2)}) copy-start(bf16[1,184,1152]{2,1,0:T(8,128)(2,1)} %reduce-scatter.35.cloned.1.call-done) | copy-start | bytes 1271812
  270.2 76.4 %reduce-scatter.37.cloned.1.call-start = ((), (), s32[]{:S(2)}) async-start(), calls=%async_computation.23 | async-start | bytes 2119680
  277.4 111.3 %all-gather.17.cloned.1.call-start = ((), (), s32[]{:S(2)}) async-start(), calls=%async_computation.15 | async-start | bytes 2119680 | tf_op jit(solution)/shard_map/all_gather | solution.py:47
  349.2 43.2 %copy-start.22 = (f32[4,736]{1,0:T(4,128)S(1)}, f32[4,736]{1,0:T(4,128)}, u32[]{:S(2)}) copy-start(f32[4,736]{1,0:T(4,128)} %copy-done.21) | copy-start | bytes 35332
  350.1 96.9 %reduce-scatter.41.cloned.1.call-start = ((), (), s32[]{:S(2)}) async-start(), calls=%async_computation.25 | async-start | bytes 2119680
  392.4 5.7 copy-start.28
  398.1 10.6 %copy-start.14 = (bf16[736,4,72]{0,2,1:T(8,128)(2,1)}, bf16[736,4,72]{0,2,1:T(8,128)(2,1)S(1)}, u32[]{:S(2)}) copy-start(bf16[736,4,72]{0,2,1:T(8,128)(2,1)S(1)} %get-tuple-element.100) | copy-start | bytes 1271812
  398.1 5.6 copy-start.10
  403.7 1.5 copy-start.8
  405.2 2.2 copy-start.11
  406.2 1.2 copy-start.5
  406.2 1.3 copy-start.4
  411.1 96.7 %reduce-scatter.33.cloned.1.call-start = ((), (), s32[]{:S(2)}) async-start(), calls=%async_computation.21 | async-start | bytes 5971968 | tf_op jit(solution)/shard_map/reduce_scatter | solution.py:238
  418.5 1.5 copy-start.26
  418.5 150.3 %reduce-scatter.31.cloned.1.call-start = ((), (), s32[]{:S(2)}) async-start(), calls=%async_computation.20 | async-start | bytes 5971968 | tf_op jit(solution)/shard_map/reduce_scatter | solution.py:237
  426.4 1.0 copy-start.17
  426.5 5.0 copy-start.15
  426.5 185.4 %reduce-scatter.29.cloned.1.call-start = ((), (), s32[]{:S(2)}) async-start(), calls=%async_computation.19 | async-start | bytes 1990656 | tf_op jit(solution)/shard_map/reduce_scatter | solution.py:236
  431.4 4.1 copy-start.6
  431.4 223.6 %reduce-scatter.27.cloned.1.call-start = ((), (), s32[]{:S(2)}) async-start(), calls=%async_computation.18 | async-start | bytes 1990656 | tf_op jit(solution)/shard_map/reduce_scatter | solution.py:235
  435.4 4.1 copy-start.12
  435.4 262.8 %reduce-scatter.23.cloned.1.call-start = ((), (), s32[]{:S(2)}) async-start(), calls=%async_computation.16 | async-start | bytes 1990656 | tf_op jit(solution)/shard_map/reduce_scatter | solution.py:233
  439.4 3.9 copy-start.23
  439.4 302.0 %reduce-scatter.25.cloned.1.call-start = ((), (), s32[]{:S(2)}) async-start(), calls=%async_computation.17 | async-start | bytes 1990656 | tf_op jit(solution)/shard_map/reduce_scatter | solution.py:234
Sparse Core Ops, SparseCore 0:
  49.1 38.4 all-gather.6
  105.9 37.5 reduce-scatter.34
  270.3 37.3 reduce-scatter.38
  309.8 36.7 reduce-scatter.36
  350.2 38.5 all-gather.16
Sparse Core Ops, SparseCore 1:
  108.2 30.3 all-gather.10
  148.2 38.3 all-gather.8
  188.1 37.8 all-gather.14
  227.8 28.9 all-gather.12
  411.2 35.8 reduce-scatter.40
  451.0 56.7 reduce-scatter.32
  512.0 56.8 reduce-scatter.30
  572.6 39.2 reduce-scatter.28
  615.7 39.2 reduce-scatter.26
  659.0 39.2 reduce-scatter.22
  702.1 39.2 reduce-scatter.24
where the time goes:
time: 754 us; the launch traced here: 749 us
  waiting for transfers between devices  490 us (65%)
  blocking collectives  110 us (15%)
  matrix products  86 us (11%)
  other arithmetic  22.3 us (3%)
  local copies, waits for them, and re-layouts  20.8 us (3%)
  between operations  17.6 us (2%)
    unnamed x20, waiting for transfers between devices  109 us
    all_gather x4, waiting for transfers between devices, gather_rows(): return lax.all_gather(local, 'tensor', axis=1, tiled=True)  108 us
    dot_general x18, matrix products, mat_dot(): return jnp.dot(left, right, preferred_element_type=jnp.float32)  68.8 us
    reduce_scatter x1, waiting for transfers between devices, shards(): lax.psum_scatter(up_grad, 'dp', scatter_dimension=0, tiled=True)  61.1 us
    reduce_scatter x1, waiting for transfers between devices, shards(): lax.psum_scatter(query_grad, 'dp', scatter_dimension=0, tiled=True)  43.2 us
    reduce_scatter x1, waiting for transfers between devices, shards(): lax.psum_scatter(value_grad, 'dp', scatter_dimension=0, tiled=True)  43.1 us
    reduce_scatter x1, waiting for transfers between devices, shards(): lax.psum_scatter(key_grad, 'dp', scatter_dimension=0, tiled=True)  43.1 us
    reduce_scatter x1, waiting for transfers between devices, shards(): lax.psum_scatter(out_grad, 'dp', scatter_dimension=1, tiled=True)  43.1 us
  transfers between devices with their start and end apart: 16, of which 14 were waited for; matrix products, arithmetic and copies ran while one was open for 8% of the time, Pallas kernels for 0%

commit v1 on v0

v1 whole, which is shorter than its diff:
```python
from functools import partial
import math

import jax
import jax.numpy as jnp
from jax import lax
from jax.experimental import pallas as pl
from jax.experimental.pallas import tpu as pltpu
from jax.sharding import PartitionSpec as P

HD = 72
EPSILON = 1e-06
GELU_COEF = 0.7978845608028654
MASK_FILL = -1e30
MESH = pl.DeviceIdType.MESH
ANY = pl.BlockSpec(memory_space=pl.ANY)
VM = pl.BlockSpec(memory_space=pltpu.VMEM)
DMA = pltpu.SemaphoreType.DMA
VMEM_BYTES = 60 << 20
F32 = jnp.float32
BF16 = jnp.bfloat16


def remote(src, dst, send_sem, recv_sem, device):
    return pltpu.make_async_remote_copy(
        src_ref=src,
        dst_ref=dst,
        send_sem=send_sem,
        recv_sem=recv_sem,
        device_id=device,
        device_id_type=MESH,
    )


class Place:
    def __init__(self, dp_size, line):
        self.dp_size, self.line, self.chips = dp_size, line, dp_size // 2
        self.dp = lax.axis_index("dp")
        self.z = lax.axis_index("tensor")
        self.core = lax.rem(self.dp, 2)
        self.chip = lax.div(self.dp, 2)
        self.sibling = (2 * self.chip + 1 - self.core, self.z)

    def chip_at(self, k):
        return lax.rem(self.chip + k + self.chips, self.chips)

    def peer(self, k):
        return (2 * self.chip_at(k) + self.core, self.z)

    def along(self, k):
        return (self.dp, lax.rem(self.z + k + self.line, self.line))

    def enter(self, across=True, line=True):
        barrier = pltpu.get_barrier_semaphore()
        devices = []
        if across:
            devices += [self.peer(k) for k in range(1, self.chips)] + [self.sibling]
        if line:
            devices += [self.along(k) for k in range(1, self.line)]
        for device in devices:
            pl.semaphore_signal(barrier, inc=1, device_id=device, device_id_type=MESH)
        pl.semaphore_wait(barrier, len(devices))


class DpGather:
    @staticmethod
    def sems(place_chips):
        return [DMA((place_chips,)), DMA((place_chips,)), DMA((2 * place_chips,)), DMA(())]

    def __init__(self, place, src, dst, sems):
        self.p, self.src, self.dst = place, src, dst
        self.across, self.inside, self.recv, self.local = sems

    def start(self):
        p = self.p
        mine = self.dst.at[p.dp]
        for k in range(1, p.chips):
            remote(self.src, mine, self.across.at[k], self.recv.at[p.dp], p.peer(k)).start()
        remote(self.src, mine, self.inside.at[0], self.recv.at[p.dp], p.sibling).start()
        pltpu.make_async_copy(self.src, mine, self.local).start()

    def forward(self):
        p = self.p
        for k in range(1, p.chips):
            slot = 2 * p.chip_at(-k) + p.core
            block = self.dst.at[slot]
            remote(block, block, self.across.at[k], self.recv.at[slot], p.sibling).wait_recv()
            remote(block, block, self.inside.at[k], self.recv.at[slot], p.sibling).start()

    def finish(self):
        p = self.p
        mine = self.dst.at[p.dp]
        for k in range(p.chips):
            slot = 2 * p.chip_at(-k) + 1 - p.core
            block = self.dst.at[slot]
            remote(block, block, self.inside.at[k], self.recv.at[slot], p.sibling).wait_recv()
        for k in range(p.chips):
            remote(self.src, mine, self.inside.at[k], self.recv.at[0], p.sibling).wait_send()
            if k > 0:
                remote(self.src, mine, self.across.at[k], self.recv.at[0], p.sibling).wait_send()
        pltpu.make_async_copy(self.src, mine, self.local).wait()


class LineGather:
    @staticmethod
    def sems(line):
        return [DMA((line,)), DMA((line,)), DMA((line,)), DMA(())]

    def __init__(self, place, src, dst, sems):
        self.p, self.src, self.dst = place, src, dst
        self.right, self.left, self.recv, self.local = sems

    def send(self, src, slot, step):
        p = self.p

        @pl.when(p.z < p.line - 1)
        def _():
            remote(src, self.dst.at[slot], self.right.at[step], self.recv.at[slot], (p.dp, p.z + 1)).start()

    def send_left(self, src, slot, step):
        p = self.p

        @pl.when(p.z > 0)
        def _():
            remote(src, self.dst.at[slot], self.left.at[step], self.recv.at[slot], (p.dp, p.z - 1)).start()

    def start(self):
        p = self.p
        self.send(self.src, p.z, 0)
        self.send_left(self.src, p.z, 0)
        pltpu.make_async_copy(self.src, self.dst.at[p.z], self.local).start()

    def arrive(self, slot):
        block = self.dst.at[slot]
        remote(block, block, self.right.at[0], self.recv.at[slot], self.p.sibling).wait_recv()

    def step(self, s):
        p = self.p

        @pl.when(p.z >= s)
        def _():
            self.arrive(p.z - s)
            self.send(self.dst.at[p.z - s], p.z - s, s)

        @pl.when(p.z + s < p.line)
        def _():
            self.arrive(p.z + s)
            self.send_left(self.dst.at[p.z + s], p.z + s, s)

    def finish(self):
        p = self.p
        block = self.dst.at[0]
        for s in range(p.line):

            @pl.when(jnp.logical_and(p.z >= s, p.z < p.line - 1))
            def _():
                remote(self.src, block, self.right.at[s], self.recv.at[0], p.sibling).wait_send()

            @pl.when(jnp.logical_and(p.z + s < p.line, p.z > 0))
            def _():
                remote(self.src, block, self.left.at[s], self.recv.at[0], p.sibling).wait_send()

        pltpu.make_async_copy(self.src, self.dst.at[p.z], self.local).wait()


class LineExchange:
    @staticmethod
    def sems(line):
        return [DMA((line,)), DMA((line,)), DMA(())]

    def __init__(self, place, src, dst, sems):
        self.p, self.src, self.dst = place, src, dst
        self.sent, self.recv, self.local = sems

    def start(self):
        p = self.p
        for k in range(1, p.line):
            to = p.along(k)
            remote(self.src.at[to[1]], self.dst.at[p.z], self.sent.at[k], self.recv.at[p.z], to).start()
        pltpu.make_async_copy(self.src.at[p.z], self.dst.at[p.z], self.local).start()

    def finish(self):
        p = self.p
        for k in range(1, p.line):
            slot = p.along(k)[1]
            block = self.dst.at[slot]
            remote(block, block, self.sent.at[k], self.recv.at[slot], p.sibling).wait_recv()
        for k in range(1, p.line):
            block = self.src.at[0]
            remote(block, block, self.sent.at[k], self.recv.at[0], p.sibling).wait_send()
        pltpu.make_async_copy(self.src.at[p.z], self.dst.at[p.z], self.local).wait()


class LineSum:
    @staticmethod
    def sems(line):
        return [DMA((line,)), DMA((line,)), DMA((line,))]

    def __init__(self, place, part, from_left, from_right, sems):
        self.p, self.part, self.from_left, self.from_right = place, part, from_left, from_right
        self.sent, self.recv_left, self.recv_right = sems

    def add(self, d, got):
        self.part[d] = (self.part[d].astype(F32) + got[d].astype(F32)).astype(BF16)

    def wait(self, got, recv, d):
        remote(got.at[d], got.at[d], self.sent.at[d], recv.at[d], self.p.sibling).wait_recv()

    def move(self, i):
        p = self.p
        d = p.line - 1 - i

        @pl.when(p.z < d)
        def _():
            @pl.when(p.z > 0)
            def _():
                self.wait(self.from_left, self.recv_left, d)
                self.add(d, self.from_left)

            remote(self.part.at[d], self.from_left.at[d], self.sent.at[d], self.recv_left.at[d], (p.dp, p.z + 1)).start()

        @pl.when(p.z > i)
        def _():
            @pl.when(p.z < p.line - 1)
            def _():
                self.wait(self.from_right, self.recv_right, i)
                self.add(i, self.from_right)

            remote(self.part.at[i], self.from_right.at[i], self.sent.at[i], self.recv_right.at[i], (p.dp, p.z - 1)).start()

    def finish(self, out):
        p = self.p
        out[...] = self.part[p.z].astype(F32)

        @pl.when(p.z > 0)
        def _():
            self.wait(self.from_left, self.recv_left, p.z)
            out[...] += self.from_left[p.z].astype(F32)

        @pl.when(p.z < p.line - 1)
        def _():
            self.wait(self.from_right, self.recv_right, p.z)
            out[...] += self.from_right[p.z].astype(F32)

        for d in range(p.line):

            @pl.when(p.z != d)
            def _():
                block = self.part.at[d]
                remote(block, block, self.sent.at[d], self.recv_left.at[d], p.sibling).wait_send()


class DpSum:
    @staticmethod
    def sems(chips):
        return [DMA((chips,)), DMA((chips,)), DMA((chips,)), DMA((chips,))]

    def __init__(self, place, part, near, far, sems):
        self.p, self.part, self.near, self.far = place, part, near, far
        self.sent, self.recv, self.sent_far, self.recv_far = sems

    def start(self):
        p = self.p
        for k in [*range(1, p.chips), 0]:
            chip = p.chip_at(k)
            remote(self.part.at[2 * chip + 1 - p.core], self.near.at[k], self.sent.at[k], self.recv.at[k], p.sibling).start()

    def wait_near(self, k):
        block = self.near.at[k]
        remote(block, block, self.sent.at[k], self.recv.at[k], self.p.sibling).wait_recv()

    def move(self):
        p = self.p
        for k in range(1, p.chips):
            slot = 2 * p.chip_at(k) + p.core
            self.wait_near(k)
            self.part[slot] = (self.part[slot].astype(F32) + self.near[k].astype(F32)).astype(BF16)
            remote(self.part.at[slot], self.far.at[k], self.sent_far.at[k], self.recv_far.at[k], p.peer(k)).start()

    def finish(self):
        p = self.p
        self.wait_near(0)
        total = self.part[p.dp].astype(F32) + self.near[0].astype(F32)
        for k in range(1, p.chips):
            block = self.far.at[k]
            remote(block, block, self.sent_far.at[k], self.recv_far.at[k], p.sibling).wait_recv()
            total += self.far[k].astype(F32)
        for k in range(p.chips):
            block = self.near.at[0]
            remote(block, block, self.sent.at[k], self.recv.at[0], p.sibling).wait_send()
            if k > 0:
                remote(block, block, self.sent_far.at[k], self.recv.at[0], p.sibling).wait_send()
        return total


def params(collective_id):
    return pltpu.CompilerParams(
        collective_id=collective_id, has_side_effects=True, vmem_limit_bytes=VMEM_BYTES
    )


def shape(*dims, dtype=BF16):
    return jax.ShapeDtypeStruct(dims, dtype)


def gather_all(sizes, across, chained, along):
    n, t = sizes
    count = (len(across), len(chained), len(along))

    def kernel(*refs):
        refs = list(refs)
        take = lambda m: [refs.pop(0) for _ in range(m)]
        a_in, c_in, l_in = take(count[0]), take(count[1]), take(count[2])
        a_out, c_out, l_out = take(count[0]), take(count[1]), take(count[2])
        c_mid = take(count[1])
        place = Place(n, t)
        dp_ops = [DpGather(place, s, d, take(4)) for s, d in zip(a_in, a_out)]
        mid_ops = [LineGather(place, s, d, take(4)) for s, d in zip(c_in, c_mid)]
        tail_ops = [DpGather(place, s, d, take(4)) for s, d in zip(c_mid, c_out)]
        line_ops = [LineGather(place, s, d, take(4)) for s, d in zip(l_in, l_out)]
        place.enter()
        for op in mid_ops + line_ops + dp_ops:
            op.start()
        for s in range(1, t):
            for op in mid_ops:
                op.step(s)
        for op in mid_ops:
            op.finish()
        for op in tail_ops:
            op.start()
        for s in range(1, t):
            for op in line_ops:
                op.step(s)
        for op in dp_ops + tail_ops:
            op.forward()
        for op in line_ops + dp_ops + tail_ops:
            op.finish()

    outs = (
        [shape(n, *a.shape, dtype=a.dtype) for a in across]
        + [shape(n, t, *a.shape, dtype=a.dtype) for a in chained]
        + [shape(t, *a.shape, dtype=a.dtype) for a in along]
    )
    scratch = [pltpu.VMEM((t, *a.shape), a.dtype) for a in chained]
    for _ in across:
        scratch += DpGather.sems(n // 2)
    for _ in chained:
        scratch += LineGather.sems(t)
    for _ in chained:
        scratch += DpGather.sems(n // 2)
    for _ in along:
        scratch += LineGather.sems(t)
    return pl.pallas_call(
        kernel,
        out_shape=outs,
        in_specs=[ANY] * sum(count),
        out_specs=[ANY] * sum(count),
        scratch_shapes=scratch,
        compiler_params=params(0),
        name="gather_all",
    )(*across, *chained, *along)


def line_gather(sizes, block, collective_id):
    n, t = sizes

    def kernel(src, dst, *sems):
        place = Place(n, t)
        op = LineGather(place, src, dst, sems)
        place.enter(across=False)
        op.start()
        for s in range(1, t):
            op.step(s)
        op.finish()

    return pl.pallas_call(
        kernel,
        out_shape=shape(t, *block.shape),
        in_specs=[ANY],
        out_specs=ANY,
        scratch_shapes=LineGather.sems(t),
        compiler_params=params(collective_id),
        name="line_gather",
    )(block)


def line_exchange(sizes, blocks, collective_id):
    n, t = sizes

    def kernel(src, dst, *sems):
        place = Place(n, t)
        op = LineExchange(place, src, dst, sems)
        place.enter(across=False)
        op.start()
        op.finish()

    return pl.pallas_call(
        kernel,
        out_shape=shape(*blocks.shape),
        in_specs=[ANY],
        out_specs=ANY,
        scratch_shapes=LineExchange.sems(t),
        compiler_params=params(collective_id),
        name="line_exchange",
    )(blocks)


def line_sum(sizes, parts, collective_id):
    n, t = sizes
    m = len(parts)

    def kernel(*refs):
        refs = list(refs)
        take = lambda c: [refs.pop(0) for _ in range(c)]
        ins, outs, work, left, right = take(m), take(m), take(m), take(m), take(m)
        place = Place(n, t)
        ops = [LineSum(place, *r, take(3)) for r in zip(work, left, right)]
        place.enter(across=False)
        for op, src in zip(ops, ins):
            op.part[...] = src[...]
        for op in ops:
            for i in range(t - 1):
                op.move(i)
        for op, out in zip(ops, outs):
            op.finish(out)

    scratch = [pltpu.VMEM(p.shape, BF16) for _ in range(3) for p in parts]
    for _ in parts:
        scratch += LineSum.sems(t)
    return pl.pallas_call(
        kernel,
        out_shape=[shape(*p.shape[1:], dtype=F32) for p in parts],
        in_specs=[VM] * m,
        out_specs=[VM] * m,
        scratch_shapes=scratch,
        compiler_params=params(collective_id),
        name="line_sum",
    )(*parts)


def sum_all(sizes, across, chained, collective_id):
    n, t = sizes
    chips = n // 2
    m, c = len(across), len(chained)

    def kernel(*refs):
        refs = list(refs)
        take = lambda q: [refs.pop(0) for _ in range(q)]
        ins, outs = take(m + c), take(m + c)
        work, near, far = take(m + c), take(m + c), take(m + c)
        mid, got = take(c), take(c)
        place = Place(n, t)
        ops = [DpSum(place, *r, take(4)) for r in zip(work, near, far)]
        tails = [LineExchange(place, s, d, take(3)) for s, d in zip(mid, got)]
        place.enter()
        order = ops[m:] + ops[:m]
        sources = ins[m:] + ins[:m]
        for op, src in zip(order, sources):
            op.part[...] = src[...]
            op.start()
        for op in order:
            op.move()
        for op, s, tail in zip(ops[m:], mid, tails):
            s[...] = op.finish().astype(BF16)
            tail.start()
        for op, out in zip(ops[:m], outs[:m]):
            out[...] = op.finish()
        for tail, d, out in zip(tails, got, outs[m:]):
            tail.finish()
            out[...] = jnp.sum(d[...].astype(F32), axis=0)

    every = [*across, *chained]
    scratch = [pltpu.VMEM(p.shape, BF16) for p in every]
    scratch += [pltpu.VMEM((chips, *p.shape[1:]), BF16) for _ in range(2) for p in every]
    scratch += [pltpu.VMEM(p.shape[1:], BF16) for _ in range(2) for p in chained]
    for _ in every:
        scratch += DpSum.sems(chips)
    for _ in chained:
        scratch += LineExchange.sems(t)
    outs = [shape(*p.shape[1:], dtype=F32) for p in across] + [shape(*p.shape[2:], dtype=F32) for p in chained]
    return pl.pallas_call(
        kernel,
        out_shape=outs,
        in_specs=[VM] * len(every),
        out_specs=[VM] * len(every),
        scratch_shapes=scratch,
        compiler_params=params(collective_id),
        name="sum_all",
    )(*every)


def vector_sum(sizes, parts, collective_id):
    n, t = sizes

    def kernel(src, out, got, mid, got_line, sent, recv, sent_line, recv_line):
        place = Place(n, t)
        barrier = pltpu.get_barrier_semaphore()
        others = [lax.rem(place.dp + k, n) for k in range(1, n)]
        devices = [(d, place.z) for d in others] + [place.along(k) for k in range(1, t)]
        for device in devices:
            pl.semaphore_signal(barrier, inc=1, device_id=device, device_id_type=MESH)
        pl.semaphore_wait(barrier, len(devices))
        for k in range(1, n):
            remote(src.at[others[k - 1]], got.at[k], sent.at[k], recv.at[k], (others[k - 1], place.z)).start()
        total = src[place.dp]
        for k in range(1, n):
            remote(got.at[k], got.at[k], sent.at[k], recv.at[k], place.sibling).wait()
            total += got[k]
        mid[...] = total
        for k in range(1, t):
            remote(mid, got_line.at[k], sent_line.at[k], recv_line.at[k], place.along(k)).start()
        for k in range(1, t):
            remote(mid, got_line.at[k], sent_line.at[k], recv_line.at[k], place.sibling).wait()
            total += got_line[k]
        out[...] = total

    block = parts.shape[1:]
    return pl.pallas_call(
        kernel,
        out_shape=shape(*block, dtype=F32),
        in_specs=[VM],
        out_specs=VM,
        scratch_shapes=[
            pltpu.VMEM((n, *block), F32),
            pltpu.VMEM(block, F32),
            pltpu.VMEM((t, *block), F32),
            DMA((n,)),
            DMA((n,)),
            DMA((t,)),
            DMA((t,)),
        ],
        compiler_params=params(collective_id),
        name="vector_sum",
    )(parts)


def norm_forward(inputs, gain_vec, shift_vec):
    centred = inputs - jnp.mean(inputs, axis=-1, keepdims=True)
    inv_std = lax.rsqrt(jnp.mean(centred * centred, axis=-1, keepdims=True) + EPSILON)
    normed = centred * inv_std
    return (normed * gain_vec + shift_vec, normed, inv_std)


def norm_backward(grad_in, normed, inv_std, gain_vec):
    scaled = grad_in * gain_vec
    return inv_std * (
        scaled
        - jnp.mean(scaled, axis=-1, keepdims=True)
        - normed * jnp.mean(scaled * normed, axis=-1, keepdims=True)
    )


def gelu_pair(pre_act):
    tanh_val = jnp.tanh(GELU_COEF * (pre_act + 0.044715 * pre_act * pre_act * pre_act))
    gelu_value = 0.5 * pre_act * (1.0 + tanh_val)
    gelu_slope = 0.5 * (1.0 + tanh_val) + 0.5 * pre_act * (
        1.0 - tanh_val * tanh_val
    ) * GELU_COEF * (1.0 + 3.0 * 0.044715 * pre_act * pre_act)
    return (gelu_value, gelu_slope)


def mat_dot(left, right):
    return jnp.dot(left, right, preferred_element_type=jnp.float32)


def attend(query, keys, values, valid):
    scores = jnp.einsum("qhd,khd->hqk", query, keys, preferred_element_type=jnp.float32)
    scores = jnp.where(valid[None, None, :] > 0, scores, MASK_FILL)
    highest = jnp.max(scores, axis=-1, keepdims=True)
    logsum = highest + jnp.log(jnp.sum(jnp.exp(scores - highest), axis=-1, keepdims=True))
    probs = jnp.exp(scores - logsum).astype(jnp.bfloat16)
    mixed = jnp.einsum("hqk,khd->qhd", probs, values, preferred_element_type=jnp.float32)
    return (mixed.astype(jnp.bfloat16), logsum[..., 0])


def attend_back(scale_factor, query, keys, values, valid, logsum, mixed, grad):
    scores = jnp.einsum("qhd,khd->hqk", query, keys, preferred_element_type=jnp.float32)
    scores = jnp.where(valid[None, None, :] > 0, scores, MASK_FILL)
    probs_full = jnp.exp(scores - logsum[:, :, None])
    probs = probs_full.astype(jnp.bfloat16)
    grad_values = jnp.einsum("hqk,qhd->khd", probs, grad, preferred_element_type=jnp.float32)
    grad_probs = jnp.einsum("qhd,khd->hqk", grad, values, preferred_element_type=jnp.float32)
    delta = jnp.sum(grad.astype(jnp.float32) * mixed.astype(jnp.float32), axis=-1).T
    grad_scores = (probs_full * (grad_probs - delta[:, :, None])).astype(jnp.bfloat16)
    grad_query = (
        jnp.einsum("hqk,khd->qhd", grad_scores, keys, preferred_element_type=jnp.float32)
        * scale_factor
    )
    grad_keys = jnp.einsum("hqk,qhd->khd", grad_scores, query, preferred_element_type=jnp.float32)
    return (grad_query, grad_keys, grad_values)


def shards(
    sizes,
    tokens,
    key_mask,
    query_weight,
    key_weight,
    value_weight,
    out_weight,
    up_weight,
    down_weight,
    first_gain,
    first_shift,
    query_bias,
    value_bias,
    out_bias,
    second_gain,
    second_shift,
    up_bias,
    down_bias,
    cotangent,
):
    n, t = sizes
    z = lax.axis_index("tensor")
    images, rows, width = tokens.shape
    share = first_gain.shape[0]
    up_share = up_bias.shape[0]
    cols = query_weight.shape[1]
    hidden_cols = up_weight.shape[1]
    heads = cols // HD
    seq = t * rows
    scale_factor = 1.0 / math.sqrt(HD)

    small = [first_gain, first_shift, query_bias, value_bias, out_bias, second_gain, second_shift, down_bias]
    pack = jnp.stack([jnp.pad(v, (0, up_share - share)) for v in small] + [up_bias])
    pack = jnp.pad(pack, ((0, 16 - len(small) - 1), (0, 0)))
    qkv_all, up_all, down_all, vec_all, out_all, token_rows, grad_rows = gather_all(
        sizes,
        [
            jnp.concatenate([query_weight, key_weight, value_weight], axis=1),
            up_weight,
            down_weight.T,
            pack,
        ],
        [out_weight.T],
        [tokens[0], cotangent[0]],
    )
    qkv_full = qkv_all.reshape(width, 3 * cols)
    up_full = up_all.reshape(width, hidden_cols)
    down_full = down_all.reshape(width, hidden_cols)
    out_full = out_all.transpose(1, 0, 2, 3).reshape(t, width, cols)
    vec = vec_all.astype(F32)
    gain_one, shift_one, query_bias_all, value_bias_all, out_bias_all, gain_two, shift_two, down_bias_all = [
        vec[:, i, :share].reshape(-1) for i in range(8)
    ]
    up_bias_all = vec[:, 8, :].reshape(-1)
    query_bias_local = lax.dynamic_slice_in_dim(query_bias_all, z * cols, cols)
    value_bias_local = lax.dynamic_slice_in_dim(value_bias_all, z * cols, cols)
    up_bias_local = lax.dynamic_slice_in_dim(up_bias_all, z * hidden_cols, hidden_cols)

    inputs = tokens[0].astype(F32)
    normed_one, inv_one = norm_forward(inputs, gain_one, shift_one)[1:]
    first = norm_forward(token_rows.reshape(seq, width).astype(F32), gain_one, shift_one)[0].astype(BF16)
    qkv = mat_dot(first, qkv_full)
    head_shape = (seq, heads, HD)
    query = ((qkv[:, :cols] + query_bias_local) * scale_factor).astype(BF16).reshape(head_shape)
    keys = qkv[:, cols : 2 * cols].astype(BF16).reshape(head_shape)
    values = (qkv[:, 2 * cols :] + value_bias_local).astype(BF16).reshape(head_shape)
    mixed, logsum = attend(query, keys, values, key_mask[0])
    mixed_rows = line_exchange(sizes, mixed.reshape(t, rows, cols), 1)
    terms = jnp.einsum("trc,tdc->trd", mixed_rows, out_full, preferred_element_type=F32).astype(BF16)
    hidden = inputs + jnp.sum(terms.astype(F32), axis=0) + out_bias_all
    second, normed_two, inv_two = norm_forward(hidden, gain_two, shift_two)
    second_all = line_gather(sizes, second.astype(BF16), 2).reshape(seq, width)
    pre_act = mat_dot(second_all, up_full) + up_bias_local
    gelu_value, gelu_slope = gelu_pair(pre_act)
    act = gelu_value.astype(BF16)
    cot_all = grad_rows.reshape(seq, width)
    out_part = mat_dot(act, down_full.T).astype(BF16)
    grad_pre = mat_dot(cot_all, down_full) * gelu_slope
    up_bias_part = jnp.sum(grad_pre, axis=0)
    grad_pre_low = grad_pre.astype(BF16)
    second_part = mat_dot(grad_pre_low, up_full.T).astype(BF16)
    grad_second, mlp_out = line_sum(
        sizes, [second_part.reshape(t, rows, width), out_part.reshape(t, rows, width)], 3
    )
    output = (hidden + mlp_out + down_bias_all).astype(BF16)
    down_grad = mat_dot(cot_all.T, act).astype(BF16)
    up_grad = mat_dot(second_all.T, grad_pre_low).astype(BF16)
    grad_out = cotangent[0].astype(F32)
    down_bias_grad = jnp.sum(grad_out, axis=0)
    second_gain_grad = jnp.sum(grad_second * normed_two, axis=0)
    second_shift_grad = jnp.sum(grad_second, axis=0)
    grad_hidden = grad_out + norm_backward(grad_second, normed_two, inv_two, gain_two)
    out_bias_grad = jnp.sum(grad_hidden, axis=0)
    hidden_low = grad_hidden.astype(BF16)
    grad_mixed_rows = jnp.einsum("rd,tdc->trc", hidden_low, out_full, preferred_element_type=F32).astype(BF16)
    out_grad = jnp.einsum("rd,trc->tdc", hidden_low, mixed_rows, preferred_element_type=F32).astype(BF16)
    grad_mixed = line_exchange(sizes, grad_mixed_rows, 4).reshape(head_shape)
    grad_query_f, grad_keys_f, grad_values_f = attend_back(
        scale_factor, query, keys, values, key_mask[0], logsum, mixed, grad_mixed
    )
    grad_query_f = grad_query_f.reshape(seq, cols)
    grad_keys_f = grad_keys_f.reshape(seq, cols)
    grad_values_f = grad_values_f.reshape(seq, cols)
    query_bias_part = jnp.sum(grad_query_f, axis=0)
    value_bias_part = jnp.sum(grad_values_f, axis=0)
    grad_qkv = jnp.concatenate([g.astype(BF16) for g in (grad_query_f, grad_keys_f, grad_values_f)], axis=1)
    first_part = mat_dot(grad_qkv, qkv_full.T).astype(BF16)
    (grad_first,) = line_sum(sizes, [first_part.reshape(t, rows, width)], 5)
    qkv_grad = mat_dot(first.T, grad_qkv).astype(BF16)
    qkv_share, up_grad_share, down_share, out_share = sum_all(
        sizes,
        [
            qkv_grad.reshape(n, share, 3 * cols),
            up_grad.reshape(n, share, hidden_cols),
            down_grad.reshape(n, share, hidden_cols),
        ],
        [out_grad.reshape(t, n, share, cols).transpose(1, 0, 2, 3)],
        6,
    )
    first_gain_grad = jnp.sum(grad_first * normed_one, axis=0)
    first_shift_grad = jnp.sum(grad_first, axis=0)
    input_grad = grad_hidden + norm_backward(grad_first, normed_one, inv_one, gain_one)
    placed = lambda part, full: lax.dynamic_update_slice_in_dim(
        jnp.zeros((full,), F32), part, z * part.shape[0], 0
    )
    wide = jnp.stack(
        [
            first_gain_grad,
            first_shift_grad,
            placed(query_bias_part, width),
            placed(value_bias_part, width),
            out_bias_grad,
            second_gain_grad,
            second_shift_grad,
            down_bias_grad,
        ]
    ).reshape(8, n, share)
    wide = jnp.pad(wide, ((0, 0), (0, 0), (0, up_share - share)))
    last = placed(up_bias_part, up_bias_all.shape[0]).reshape(1, n, up_share)
    wide = jnp.pad(jnp.concatenate([wide, last]), ((0, 7), (0, 0), (0, 0))).transpose(1, 0, 2)
    vectors = vector_sum(sizes, wide, 7)
    outs = [vectors[i, :share] for i in range(8)]
    return (
        output[None],
        input_grad[None],
        qkv_share[:, :cols],
        qkv_share[:, cols : 2 * cols],
        qkv_share[:, 2 * cols :],
        out_share.T,
        up_grad_share,
        down_share.T,
        outs[0],
        outs[1],
        outs[2],
        outs[3],
        outs[4],
        outs[5],
        outs[6],
        vectors[8, :],
        outs[7],
    )


def solution(mesh):
    sizes = (mesh.shape["dp"], mesh.shape["tensor"])
    split = P("dp", "tensor")
    return jax.shard_map(
        partial(shards, sizes),
        mesh=mesh,
        in_specs=(P("dp", "tensor", None), P("dp", None), split, split, split, P("tensor", "dp"), split, P("tensor", "dp"))
        + (P("dp"),) * 9
        + (P("dp", "tensor", None),),
        out_specs=(P("dp", "tensor", None), P("dp", "tensor", None), split, split, split, P("tensor", "dp"), split, P("tensor", "dp"))
        + (P("dp"),) * 9,
        check_vma=False,
    )
```

time: 754 us -> 524 us (0.69)
  waiting for transfers between devices: 490 us -> 0 us
  Pallas kernels: 0 us -> 329 us
  blocking collectives: 110 us -> 0 us
  local copies, waits for them, and re-layouts: 20.8 us -> 90.1 us
  matrix products: 86 us -> 64.1 us
  between operations: 17.6 us -> 1.86 us
    pallas_call x0 -> x8, Pallas kernels: none -> 329 us  [the longest x2 107 us: line_sum(): pl.pallas_call(kernel, out_shape=[shape(*p.shape[1:], dtype=F32) for p in...]
    reduce_scatter x6 -> x0, waiting for transfers between devices: 243 us -> none  [the longest x1 61.1 us: shards(): lax.psum_scatter(up_grad, 'dp', scatter_dimension=0, tiled=True)]
    all_gather x6 -> x0, waiting for transfers between devices: 139 us -> none  [the longest x4 108 us: gather_rows(): return lax.all_gather(local, 'tensor', axis=1, tiled=True)]
    unnamed x20 -> x0, waiting for transfers between devices: 109 us -> none
    all_gather x4 -> x0, blocking collectives: 42.4 us -> none  [the longest x1 11.8 us: shards(): lax.all_gather(out_weight, 'dp', axis=1, tiled=True)]
    psum x1 -> x0, blocking collectives: 41.8 us -> none  [shards(): lax.psum((first_gain_grad, first_shift_grad, query_bias_full, value_bias_...]
    dot_general x18 -> x9, matrix products: 68.8 us -> 37.3 us  [mat_dot(): return jnp.dot(left, right, preferred_element_type=jnp.float32)]
    unnamed x1 -> x0, blocking collectives: 26.1 us -> none
  transfers between devices with their start and end apart: 16 -> 0, of which waited for: 14 -> 0; matrix products, arithmetic and copies ran while one was open for 8% -> 0% of each run, Pallas kernels for 0% -> 0%
where the time goes in v1:
time: 524 us; the launch traced here: 514 us
  Pallas kernels  329 us (63%)
  local copies, waits for them, and re-layouts  90.1 us (17%)
  matrix products  64.1 us (12%)
  other arithmetic  29.1 us (6%)
    pallas_call x2, Pallas kernels, line_sum(): pl.pallas_call(kernel, out_shape=[shape(*p.shape[1:], dtype=F32) for p in...  107 us
    pallas_call x1, Pallas kernels, gather_all(): pl.pallas_call(kernel, out_shape=outs, in_specs=[ANY] * sum(count), out_s...  78 us
    pallas_call x1, Pallas kernels, sum_all(): pl.pallas_call(kernel, out_shape=outs, in_specs=[VM] * len(every), out_sp...  72.7 us
    dot_general x9, matrix products, mat_dot(): return jnp.dot(left, right, preferred_element_type=jnp.float32)  37.3 us
    pallas_call x1, Pallas kernels, line_gather(): pl.pallas_call(kernel, out_shape=shape(t, *block.shape), in_specs=[ANY],...  33.6 us
    pallas_call x2, Pallas kernels, line_exchange(): pl.pallas_call(kernel, out_shape=shape(*blocks.shape), in_specs=[ANY], ou...  23.4 us
    another operation x13, local copies, waits for them, and re-layouts, shards(): jnp.stack([first_gain_grad, first_shift_grad, placed(query_bias_part, wid...  16.5 us
    unnamed x103, local copies, waits for them, and re-layouts  14.3 us

profile of v1, /device:TPU:0, one launch (start us, length us, event | category | flops | bytes accessed | tf_op | source)
XLA Modules:
  0.0 514.0 jit_solution(18135280868914126188)
XLA Ops:
  0.7 1.8 pad_maximum_fusion.3.refs_0_
  9.2 78.0 %gather_all.1 = (bf16[8,144,864]{2,1,0:T(8,128)(2,1)}, bf16[8,144,1076]{2,1,0:T(8,128)(2,1)}, bf16[8,144,1076]{2,1,0:T(8,128)(2,1)}, bf16[8,16,538]{2,1,0:T(8,12...) custom-call(bf16[144,864]{1,0:T(8,128)(2,1)} %pad_maximum_fusion.3.refs_0_, ...), custom_call_target="tpu_custom_call" | custom-call | tf_op jit(solution)/shard_map/gather_all/pallas_call | solution.py:353
  87.2 1.9 convert_reduce_fusion.1
  89.1 2.1 multiply_reduce_fusion
  93.2 2.1 fusion.47
  95.3 1.5 copy-done.12
  96.7 1.4 fusion.41
  100.9 2.7 slice.120
  104.9 1.7 select_reduce_fusion
  106.7 1.8 exponential_reduce_fusion
  108.4 1.7 copy-done
  110.1 2.6 copy.96
  115.0 6.2 %fusion.13 = bf16[736,4,72]{0,2,1:T(8,128)(2,1)} fusion(bf16[736,4,72]{0,2,1:T(8,128)(2,1)S(1)} %bitcast.139, f32[4,736,736]{1,2,0:T(8,128)} %copy-done, f32[4,736]{1,0:T(4,128)S(1)} %log_add_fusion, pred[736]{0:T(1024)(128)(4,1)S(1)} %compare_reduce_fusion), kind=kOutput, calls=%fused_computation.45 | convolution fusion | flops 318729216 | bytes 9527520 | tf_op jit(solution)/shard_map/hqk,khd->qhd/dot_general | solution.py:572
  121.1 1.5 reshape.248
  122.6 1.8 copy.75.src
  124.4 14.0 %line_exchange.2 = bf16[4,184,288]{2,1,0:T(8,128)(2,1)} custom-call(bf16[4,184,288]{2,1,0:T(8,128)(2,1)} %copy.75.src), custom_call_target="tpu_custom_call" | custom-call | tf_op jit(solution)/shard_map/line_exchange/pallas_call | solution.py:397
  138.4 2.4 copy.76
  140.8 1.7 copy-done.2
  142.5 2.3 convert_reduce_fusion
  145.1 1.5 fusion.39
  148.7 33.6 %line_gather.1 = bf16[4,184,1152]{2,1,0:T(8,128)(2,1)} custom-call(bf16[184,1152]{1,0:T(8,128)(2,1)} %add_convert_fusion.3.src), custom_call_target="tpu_custom_call" | custom-call | tf_op jit(solution)/shard_map/line_gather/pallas_call | solution.py:376
  183.4 4.9 convolution_add_fusion
  188.3 4.4 convolution_convert_fusion.5
  192.8 5.7 %fusion.46 = (f32[1076]{0:T(1024)}, bf16[736,1076]{0,1:T(8,128)(2,1)S(1)}) fusion(f32[736,1076]{0,1:T(8,128)S(1)} %convolution_add_fusion, bf16[736,1152]{1,0:T(8,128)(2,1)S(1)} %bitcast.161, bf16[1152,1076]{1,0:T(8,128)(2,1)S(1)} %bitcast.158), kind=kOutput, calls=%fused_computation.115 | convolution fusion | flops 1840458240 | bytes 8930768 | tf_op jit(solution)/shard_map/dot_general | solution.py:563
  198.5 3.9 convolution_convert_fusion.6
  202.4 67.4 %line_sum.2 = (f32[184,1152]{1,0:T(8,128)}, f32[184,1152]{1,0:T(8,128)}) custom-call(bf16[4,184,1152]{2,1,0:T(8,128)(2,1)} %bitcast.132, bf16[4,184,1152]{2,1,0:T(8,128)(2,1)} %bitcast.131), custom_call_target="tpu_custom_call" | custom-call | tf_op jit(solution)/shard_map/line_sum/pallas_call | solution.py:430
  269.8 2.2 multiply_reduce_fusion.2
  272.1 3.5 fusion.38
  276.6 1.7 fusion.12.src
  278.3 9.5 %line_exchange.3 = bf16[4,184,288]{2,1,0:T(8,128)(2,1)} custom-call(bf16[4,184,288]{2,1,0:T(8,128)(2,1)} %fusion.12.src), custom_call_target="tpu_custom_call" | custom-call | tf_op jit(solution)/shard_map/line_exchange/pallas_call | solution.py:397
  287.8 2.0 copy.79
  292.3 6.6 %multiply_convert_fusion = bf16[4,736,736]{1,2,0:T(8,128)(2,1)S(1)} fusion(f32[4,736,736]{1,2,0:T(8,128)} %copy-done, f32[4,736]{1,0:T(4,128)S(1)} %bitcast.146, f32[4,736]{1,0:T(4,128)S(1)} %log_add_fusion, pred[736]{0:T(1024)(128)(4,1)S(1)} %compare_reduce_fusion, bf16[736,4,72]{0,2,1:T(8,128)(2,1)} %reshape.256, bf16[736,4,72]{0,2,1:T(8,128)(2,1)} %bitcast.140), kind=kOutput, calls=%fused_computation | convolution fusion | flops 322850816 | bytes 13872864 | tf_op jit(solution)/shard_map/qhd,khd->hqk/dot_general | solution.py:582
  298.9 1.6 fusion.43
  300.5 1.4 convolution_convert_fusion.9
  302.0 2.7 fusion.42
  304.7 3.4 convolution_convert_fusion.4
  308.0 39.9 %line_sum.3 = f32[184,1152]{1,0:T(8,128)} custom-call(bf16[4,184,1152]{2,1,0:T(8,128)(2,1)} %bitcast.133), custom_call_target="tpu_custom_call" | custom-call | tf_op jit(solution)/shard_map/line_sum/pallas_call | solution.py:430
  348.0 2.2 fusion.24
  350.2 1.4 stack.73
  351.6 1.4 stack.74
  354.9 1.5 dynamic_update_slice.11
  357.7 1.4 stack.77
  359.1 1.4 stack.78
  363.7 1.4 stack.79
  365.1 1.4 stack.80
  366.5 1.4 stack.83
  367.9 1.4 stack.81
  369.2 1.4 stack.82
  370.6 1.5 stack.84
  372.8 1.5 dynamic_update_slice.13
  374.2 1.4 reshape.262
  377.3 13.8 %vector_sum.1 = f32[16,538]{1,0:T(8,128)} custom-call(f32[8,16,538]{2,1,0:T(8,128)} %pad_bitcast_fusion.src), custom_call_target="tpu_custom_call" | custom-call | tf_op jit(solution)/shard_map/vector_sum/pallas_call | solution.py:518
  391.1 1.6 fusion.45
  394.0 2.6 fusion.5
  396.6 4.7 copy.87
  401.3 4.3 copy.99
  405.6 3.8 convolution_convert_fusion.1
  409.5 5.2 %copy.85 = bf16[1152,1076]{1,0:T(8,128)(2,1)} copy(bf16[1152,1076]{0,1:T(8,128)(2,1)} %convolution_convert_fusion.1) | data formatting | bytes 4958208 | tf_op jit(solution)/shard_map/convert_element_type | solution.py:680
  416.0 3.2 convolution_convert_fusion.3
  419.2 4.2 copy.84
  423.4 5.9 %convolution_convert_fusion = bf16[1152,1076]{0,1:T(8,128)(2,1)} fusion(bf16[736,1152]{1,0:T(8,128)(2,1)S(1)} %bitcast.162, f32[736,1076]{0,1:T(8,128)} %copy-done.43), kind=kOutput, calls=%fused_computation.4 | convolution fusion | flops 1832987520 | bytes 7342592 | tf_op jit(solution)/shard_map/dot_general | solution.py:563
  429.4 5.5 %copy.86 = bf16[1152,1076]{1,0:T(8,128)(2,1)} copy(bf16[1152,1076]{0,1:T(8,128)(2,1)} %convolution_convert_fusion) | data formatting | bytes 4958208 | tf_op jit(solution)/shard_map/convert_element_type | solution.py:679
  434.9 72.7 %sum_all.1 = (f32[144,864]{1,0:T(8,128)}, f32[144,1076]{1,0:T(8,128)}, f32[144,1076]{1,0:T(8,128)}, f32[144,288]{1,0:T(8,128)}) custom-call(bf16[8,144,864]{2,1,0:T(8,128)(2,1)} %bitcast.123, bf16[8,144,1076]{2,1,0:T(8,128)(2,1)} %bitcast.120, bf16[8,144,1076]{2,1,0:T(8,128)(2,1)} %bitcast.121, bf16[8,4,144,288]{3,2,1,0:T(8,128)(2,1)} %bitcast.119), custom_call_target="tpu_custom_call" | custom-call | tf_op jit(solution)/shard_map/sum_all/pallas_call | solution.py:481
  507.6 2.2 fusion.44
  (168 shorter events, 36.8 us)
Async XLA Ops:
  87.2 4.0 copy-start.24
  87.2 4.4 copy-start.1
  91.1 4.1 copy-start.25
  91.2 4.0 copy-start.19
  91.6 1.6 copy-start.37
  95.2 1.5 copy-start.12
  98.2 6.7 %copy-start.34 = (s32[1,736]{1,0:T(1,128)S(1)}, s32[1,736]{1,0:T(1,128)}, u32[]{:S(2)}) copy-start(s32[1,736]{1,0:T(1,128)} %param.19) | copy-start | bytes 8836
  100.9 5.7 %copy-start.10 = (bf16[736,288]{0,1:T(8,128)(2,1)}, bf16[736,288]{0,1:T(8,128)(2,1)S(1)}, u32[]{:S(2)}) copy-start(bf16[736,288]{0,1:T(8,128)(2,1)S(1)} %multiply_convert_fusion.2) | copy-start | bytes 1271812
  106.6 3.5 copy-start
  114.2 0.8 copy-start.20
  138.3 4.2 copy-start.8
  140.8 1.7 copy-start.2
  140.8 4.2 copy-start.4
  145.1 37.1 %copy-start.27 = (f32[184]{0:T(256)}, f32[184]{0:T(256)S(1)}, u32[]{:S(2)}) copy-start(f32[184]{0:T(256)S(1)} %broadcast_multiply_fusion.3) | copy-start | bytes 2212
  183.4 4.9 copy-start.36
  188.3 4.5 copy-start.43
  188.3 4.5 copy-start.39
  192.8 5.7 %copy-start.35 = (bf16[8,144,1076]{2,1,0:T(8,128)(2,1)S(1)}, bf16[8,144,1076]{2,1,0:T(8,128)(2,1)}, u32[]{:S(2)}) copy-start(bf16[8,144,1076]{2,1,0:T(8,128)(2,1)} %get-tuple-element.36) | copy-start | bytes 7437316
  198.5 3.9 copy-start.44
  272.1 4.5 copy-start.3
  275.7 0.9 copy-start.5
  292.2 9.7 %slice-start = ((s8[9043968]{0:T(1024)(128)(4,1)}), s8[4194304]{0:T(1024)(128)(4,1)S(1)}, s32[]{:S(2)}) async-start(s8[9043968]{0:T(1024)(128)(4,1)} %bitcast.114), calls=%async_computation | async-start | bytes 8388608
  292.2 9.7 %slice-start.1 = ((s8[9043968]{0:T(1024)(128)(4,1)}), s8[655360]{0:T(1024)(128)(4,1)S(1)}, s32[]{:S(2)}) async-start(s8[9043968]{0:T(1024)(128)(4,1)} %bitcast.114), calls=%async_computation.1 | async-start | bytes 1310720
  298.9 1.6 copy-start.11
  298.9 3.1 slice-start.2
  300.5 4.2 copy-start.15
  300.5 1.5 copy-start.13
  301.9 2.7 copy-start.21
  302.0 2.7 copy-start.38
  304.6 3.4 copy-start.41
  304.7 43.3 %copy-start.28 = (f32[184]{0:T(256)S(1)}, f32[184]{0:T(256)}, u32[]{:S(2)}) copy-start(f32[184]{0:T(256)} %copy-done.27) | copy-start | bytes 2212
  304.7 43.3 %copy-start.30 = (f32[184]{0:T(256)S(1)}, f32[184]{0:T(256)}, u32[]{:S(2)}) copy-start(f32[184]{0:T(256)} %get-tuple-element.89) | copy-start | bytes 2212
  308.0 86.0 %copy-start.6 = (f32[184,1152]{1,0:T(8,128)S(1)}, f32[184,1152]{1,0:T(8,128)}, u32[]{:S(2)}) copy-start(f32[184,1152]{1,0:T(8,128)} %copy-done.5) | copy-start | bytes 2543620
  308.0 86.0 %copy-start.9 = (bf16[4,184,288]{2,1,0:T(8,128)(2,1)S(1)}, bf16[4,184,288]{2,1,0:T(8,128)(2,1)}, u32[]{:S(2)}) copy-start(bf16[4,184,288]{2,1,0:T(8,128)(2,1)} %line_exchange.2) | copy-start | bytes 1271812
  401.3 4.3 copy-start.14
  401.3 4.3 copy-start.45
  409.5 5.3 %copy-start.26 = (f32[4,184]{1,0:T(4,128)S(1)}, f32[4,184]{1,0:T(4,128)}, u32[]{:S(2)}) copy-start(f32[4,184]{1,0:T(4,128)} %copy-done.25) | copy-start | bytes 8836
  409.5 6.1 %copy-start.16 = (bf16[736,4,72]{0,2,1:T(8,128)(2,1)S(1)}, bf16[736,4,72]{0,2,1:T(8,128)(2,1)}, u32[]{:S(2)}) copy-start(bf16[736,4,72]{0,2,1:T(8,128)(2,1)} %copy-done.15) | copy-start | bytes 1271812
  414.9 1.0 copy-start.22
  414.9 1.2 copy-start.42
  419.2 4.2 copy-start.40
  434.8 75.0 %copy-start.33 = (f32[184]{0:T(256)S(1)}, f32[184]{0:T(256)}, u32[]{:S(2)}) copy-start(f32[184]{0:T(256)} %get-tuple-element.46) | copy-start | bytes 2212
  434.8 75.0 %copy-start.32 = (f32[184]{0:T(256)S(1)}, f32[184]{0:T(256)}, u32[]{:S(2)}) copy-start(f32[184]{0:T(256)} %get-tuple-element.47) | copy-start | bytes 2212
  434.8 75.0 %copy-start.7 = (f32[184,1152]{1,0:T(8,128)S(1)}, f32[184,1152]{1,0:T(8,128)}, u32[]{:S(2)}) copy-start(f32[184,1152]{1,0:T(8,128)} %line_sum.3) | copy-start | bytes 2543620
  434.9 75.0 %copy-start.29 = (f32[184]{0:T(256)S(1)}, f32[184]{0:T(256)}, u32[]{:S(2)}) copy-start(f32[184]{0:T(256)} %copy-done.27) | copy-start | bytes 2212
  434.9 75.0 %copy-start.31 = (f32[184]{0:T(256)S(1)}, f32[184]{0:T(256)}, u32[]{:S(2)}) copy-start(f32[184]{0:T(256)} %get-tuple-element.89) | copy-start | bytes 2212
  507.6 3.6 copy-start.23
  507.6 4.3 copy-start.18
  507.6 5.1 copy-start.17

commit v2 on v0

v2 whole, which is shorter than its diff:
```python
from functools import partial
import math

import jax
import jax.numpy as jnp
from jax import lax
from jax.experimental import pallas as pl
from jax.experimental.pallas import tpu as pltpu
from jax.sharding import PartitionSpec as P

HD = 72
EPSILON = 1e-06
GELU_COEF = 0.7978845608028654
MASK_FILL = -1e30
MESH = pl.DeviceIdType.MESH
ANY = pl.BlockSpec(memory_space=pl.ANY)
VM = pl.BlockSpec(memory_space=pltpu.VMEM)
DMA = pltpu.SemaphoreType.DMA
VMEM_BYTES = 60 << 20
F32 = jnp.float32
BF16 = jnp.bfloat16


def remote(src, dst, send_sem, recv_sem, device):
    return pltpu.make_async_remote_copy(
        src_ref=src,
        dst_ref=dst,
        send_sem=send_sem,
        recv_sem=recv_sem,
        device_id=device,
        device_id_type=MESH,
    )


class Place:
    def __init__(self, dp_size, line):
        self.dp_size, self.line, self.chips = dp_size, line, dp_size // 2
        self.dp = lax.axis_index("dp")
        self.z = lax.axis_index("tensor")
        self.core = lax.rem(self.dp, 2)
        self.chip = lax.div(self.dp, 2)
        self.sibling = (2 * self.chip + 1 - self.core, self.z)

    def chip_at(self, k):
        return lax.rem(self.chip + k + self.chips, self.chips)

    def peer(self, k):
        return (2 * self.chip_at(k) + self.core, self.z)

    def along(self, k):
        return (self.dp, lax.rem(self.z + k + self.line, self.line))

    def enter(self, across=True, line=True, every=False):
        barrier = pltpu.get_barrier_semaphore()
        devices = []
        if every:
            devices += [(lax.rem(self.dp + k, self.dp_size), self.z) for k in range(1, self.dp_size)]
        elif across:
            devices += [self.peer(k) for k in range(1, self.chips)] + [self.sibling]
        if line:
            devices += [self.along(k) for k in range(1, self.line)]
        for device in devices:
            pl.semaphore_signal(barrier, inc=1, device_id=device, device_id_type=MESH)
        pl.semaphore_wait(barrier, len(devices))


class DpGather:
    @staticmethod
    def sems(chips):
        return [DMA((chips,)), DMA((chips,)), DMA((2 * chips,)), DMA(())]

    def __init__(self, place, src, dst, sems, at=None):
        self.p, self.src, self.dst = place, src, dst
        self.across, self.inside, self.recv, self.local = sems
        self.at = at if at is not None else (lambda slot: dst.at[slot])

    def start(self):
        p = self.p
        mine = self.at(p.dp)
        for k in range(1, p.chips):
            remote(self.src, mine, self.across.at[k], self.recv.at[p.dp], p.peer(k)).start()
        remote(self.src, mine, self.inside.at[0], self.recv.at[p.dp], p.sibling).start()
        pltpu.make_async_copy(self.src, mine, self.local).start()

    def forward(self):
        p = self.p
        for k in range(1, p.chips):
            slot = 2 * p.chip_at(-k) + p.core
            block = self.at(slot)
            remote(block, block, self.across.at[k], self.recv.at[slot], p.sibling).wait_recv()
            remote(block, block, self.inside.at[k], self.recv.at[slot], p.sibling).start()

    def finish(self):
        p = self.p
        mine = self.at(p.dp)
        for k in range(p.chips):
            slot = 2 * p.chip_at(-k) + 1 - p.core
            block = self.at(slot)
            remote(block, block, self.inside.at[k], self.recv.at[slot], p.sibling).wait_recv()
        for k in range(p.chips):
            remote(self.src, mine, self.inside.at[k], self.recv.at[0], p.sibling).wait_send()
            if k > 0:
                remote(self.src, mine, self.across.at[k], self.recv.at[0], p.sibling).wait_send()
        pltpu.make_async_copy(self.src, mine, self.local).wait()


class LineGather:
    @staticmethod
    def sems(line, many=()):
        return [DMA((*many, line)), DMA((*many, line)), DMA((*many, line))]

    def __init__(self, place, dst, sems, rows=None):
        self.p, self.dst = place, dst
        self.right, self.left, self.recv = sems
        self.at = (lambda slot: dst.at[slot]) if rows is None else (lambda slot: dst.at[slot, pl.ds(0, rows)])

    def send_right(self, slot):
        p = self.p
        block = self.at(slot)

        @pl.when(p.z < p.line - 1)
        def _():
            remote(block, block, self.right.at[slot], self.recv.at[slot], (p.dp, p.z + 1)).start()

    def send_left(self, slot):
        p = self.p
        block = self.at(slot)

        @pl.when(p.z > 0)
        def _():
            remote(block, block, self.left.at[slot], self.recv.at[slot], (p.dp, p.z - 1)).start()

    def start(self):
        self.send_right(self.p.z)
        self.send_left(self.p.z)

    def arrive(self, slot):
        block = self.at(slot)
        remote(block, block, self.right.at[slot], self.recv.at[slot], self.p.sibling).wait_recv()

    def relay(self, slot):
        p = self.p

        @pl.when(jnp.logical_and(p.z > slot, slot >= 0))
        def _():
            self.arrive(slot)
            self.send_right(slot)

        @pl.when(jnp.logical_and(p.z < slot, slot < p.line))
        def _():
            self.arrive(slot)
            self.send_left(slot)

    def step(self, s):
        self.relay(self.p.z - s)
        self.relay(self.p.z + s)

    def finish(self):
        p = self.p
        for slot in range(p.line):
            block = self.at(slot)

            @pl.when(jnp.logical_and(p.z >= slot, p.z < p.line - 1))
            def _():
                remote(block, block, self.right.at[slot], self.recv.at[slot], p.sibling).wait_send()

            @pl.when(jnp.logical_and(p.z <= slot, p.z > 0))
            def _():
                remote(block, block, self.left.at[slot], self.recv.at[slot], p.sibling).wait_send()


class DirectGather:
    @staticmethod
    def sems(line, many=()):
        return [DMA((*many, line)), DMA((*many, line))]

    def __init__(self, place, dst, sems):
        self.p, self.dst = place, dst
        self.sent, self.recv = sems

    def start(self):
        p = self.p
        block = self.dst.at[p.z]
        for k in range(1, p.line):
            remote(block, block, self.sent.at[k], self.recv.at[p.z], p.along(k)).start()

    def finish(self):
        p = self.p
        for k in range(1, p.line):
            slot = p.along(k)[1]
            block = self.dst.at[slot]
            remote(block, block, self.sent.at[k], self.recv.at[slot], p.sibling).wait()


class LineExchange:
    @staticmethod
    def sems(line):
        return [DMA((line,)), DMA((line,)), DMA(())]

    def __init__(self, place, src, dst, sems):
        self.p, self.src, self.dst = place, src, dst
        self.sent, self.recv, self.local = sems

    def start(self):
        p = self.p
        for k in range(1, p.line):
            to = p.along(k)
            remote(self.src.at[to[1]], self.dst.at[p.z], self.sent.at[k], self.recv.at[p.z], to).start()
        pltpu.make_async_copy(self.src.at[p.z], self.dst.at[p.z], self.local).start()

    def finish(self):
        p = self.p
        for k in range(1, p.line):
            slot = p.along(k)[1]
            block = self.dst.at[slot]
            remote(block, block, self.sent.at[k], self.recv.at[slot], p.sibling).wait_recv()
        for k in range(1, p.line):
            block = self.src.at[0]
            remote(block, block, self.sent.at[k], self.recv.at[0], p.sibling).wait_send()
        pltpu.make_async_copy(self.src.at[p.z], self.dst.at[p.z], self.local).wait()


def params(collective_id):
    return pltpu.CompilerParams(
        collective_id=collective_id, has_side_effects=True, vmem_limit_bytes=VMEM_BYTES
    )


def shape(*dims, dtype=BF16):
    return jax.ShapeDtypeStruct(dims, dtype)


def pad_to(count, unit):
    return -(-count // unit) * unit


def normalize(x):
    centred = x - jnp.mean(x, axis=-1, keepdims=True)
    inv_std = lax.rsqrt(jnp.mean(centred * centred, axis=-1, keepdims=True) + EPSILON)
    return centred * inv_std, inv_std


def dot(left, right, contract):
    return lax.dot_general(left, right, ((contract[:1], contract[1:]), ((), ())), preferred_element_type=F32)


NN, NT, TN = (1, 0), (1, 1), (0, 0)


class Dims:
    def __init__(self, sizes, rows, width, share, cols, hidden, up_share):
        self.n, self.t = sizes
        self.rows, self.width, self.share, self.cols = rows, width, share, cols
        self.hidden, self.up_share = hidden, up_share
        self.heads = cols // HD
        self.block = pad_to(rows, 16)
        self.sent_rows = rows if rows % 8 == 0 else self.block
        self.seq = self.t * self.block
        self.hidden_pad = pad_to(hidden, 128)
        self.vec_lanes = pad_to(max(up_share, share), 128)
        self.packed = self.block // self.t
        self.chunk = 32 if self.block % 32 == 0 else 16


def both_sides(place, s, work):
    def side(i, carry):
        slot = place.z - s + 2 * s * i

        @pl.when(jnp.logical_and(slot >= 0, slot < place.line))
        def _():
            work(slot)

        return carry

    lax.fori_loop(0, 2, side, 0)


def chunks(d, work):
    def one(i, carry):
        work(pl.ds(pl.multiple_of(i * d.chunk, d.chunk), d.chunk))
        return carry

    lax.fori_loop(0, d.block // d.chunk, one, 0)


def valid_keys(d, count):
    lane = lax.broadcasted_iota(jnp.int32, (1, d.seq), 1)
    zero = jnp.zeros((1, d.seq), jnp.int32)
    blk = sum([(lane >= d.block * i).astype(jnp.int32) for i in range(1, d.t)], zero)
    off = lane - blk * d.block
    inside = jnp.logical_and(off < d.rows, (off + blk * d.rows).astype(F32) < count)
    return jnp.where(inside, 1.0, 0.0)


class LineChain:
    @staticmethod
    def sems(line):
        return [DMA((line,)), DMA((line + 1,))]

    def __init__(self, place, part, inbox, sems):
        self.p, self.part, self.inbox = place, part, inbox
        self.sent, self.recv = sems

    def wait(self, slot):
        block = self.inbox.at[slot]
        remote(block, block, self.sent.at[0], self.recv.at[slot], self.p.sibling).wait_recv()

    def right(self, src, d):
        p = self.p
        remote(src.at[d], self.inbox.at[d], self.sent.at[d], self.recv.at[d], (p.dp, p.z + 1)).start()

    def left(self, src, d):
        p = self.p
        slot = jnp.where(d == p.z - 1, p.line, d)
        remote(src.at[d], self.inbox.at[slot], self.sent.at[d], self.recv.at[slot], (p.dp, p.z - 1)).start()

    def launch_right(self, d):
        @pl.when(self.p.z == 0)
        def _():
            self.right(self.part, d)

    def launch_left(self, d):
        @pl.when(self.p.z == self.p.line - 1)
        def _():
            self.left(self.part, d)

    def relay_right(self, d):
        p = self.p

        @pl.when((p.z > 0) & (p.z < d) & (d < p.line))
        def _():
            self.wait(d)
            self.inbox[d] = (self.inbox[d].astype(F32) + self.part[d].astype(F32)).astype(BF16)
            self.right(self.inbox, d)

    def relay_left(self, d):
        p = self.p

        @pl.when((p.z < p.line - 1) & (p.z > d) & (d >= 0))
        def _():
            self.wait(d)
            self.inbox[d] = (self.inbox[d].astype(F32) + self.part[d].astype(F32)).astype(BF16)
            self.left(self.inbox, d)

    def hop(self, h, d):
        p = self.p

        @pl.when(p.z == h)
        def _():
            self.relay_right(d)

        @pl.when(p.z == p.line - 1 - h)
        def _():
            self.relay_left(d)

    def tick_far(self, i):
        p = self.p
        self.relay_right(p.line - 1 + p.z - i)
        self.relay_left(i - p.line + 1 + p.z)

    def finish(self, out, rows):
        p = self.p
        out[rows, :] = self.part[p.z].astype(F32)

        @pl.when(p.z > 0)
        def _():
            self.wait(p.z)
            out[rows, :] += self.inbox[p.z].astype(F32)

        @pl.when(p.z < p.line - 1)
        def _():
            self.wait(p.line)
            out[rows, :] += self.inbox[p.line].astype(F32)

        for d in range(p.line):

            @pl.when(p.z != d)
            def _():
                block = self.part.at[d]
                remote(block, block, self.sent.at[d], self.recv.at[d], p.sibling).wait_send()


def halves(d):
    cut = pad_to(d.sent_rows // 2, 16)
    return ((0, cut), (cut, d.sent_rows - cut))


def gelu_both(u):
    square = u * u
    tanh_val = jnp.tanh(GELU_COEF * (u + 0.044715 * u * square))
    half = 0.5 * (1.0 + tanh_val)
    slope = half + 0.5 * u * (1.0 - tanh_val * tanh_val) * (GELU_COEF * (1.0 + 3.0 * 0.044715 * square))
    return u * half, slope


def forward(d, args):
    n, t, R, D, HP = d.n, d.t, d.block, d.width, d.hidden_pad
    chips = n // 2
    per_line = n // t
    scale_factor = 1.0 / math.sqrt(HD)
    split = halves(d)

    def kernel(*refs):
        refs = list(refs)
        take = lambda m: [refs.pop(0) for _ in range(m)]
        tok, cot_in, mask, wq, wk, wv, wo, wu, wd = take(9)
        vecs = take(9)
        vec, hidden, mixed_rows, grad_second, bias_part = take(5)
        kept_out = take(10)
        kept = take(10)
        qh, kh, vh, mix, probs, first, wqkv, out_t, grads, o_part = kept
        tokbuf, w_st, o_mid, o_pack, u_st, d_st, v_st, v_all = take(8)
        mixbuf, second, cot, up, down, act, pre_grad, part, inbox, upb, total = take(11)
        place = Place(n, t)
        z = place.z
        rows_of = lambda ref: (lambda slot: ref.at[pl.ds(pl.multiple_of(slot * d.share, 8), d.share)])
        g_vec = DpGather(place, v_st, v_all, take(4))
        g_qkv = DpGather(place, w_st, wqkv, take(4), rows_of(wqkv))
        g_up = DpGather(place, u_st, up, take(4), rows_of(up))
        g_down = DpGather(place, d_st, down, take(4), rows_of(down))
        g_out = DpGather(place, o_pack, out_t, take(4), rows_of(out_t))
        l_tok = LineGather(place, tokbuf, take(3), d.sent_rows)
        l_out = DirectGather(place, o_mid, take(2))
        l_cot = LineGather(place, cot, take(3), d.sent_rows)
        mix_sems = take(2)
        l_mix = lambda r: DirectGather(place, mixbuf.at[r], [sem.at[r] for sem in mix_sems])
        view = lambda ref, lo, m: ref.at[:, pl.ds(lo, m)]
        chains = [LineChain(place, view(part, *h), view(inbox, *h), take(2)) for h in split]
        (kept_sems,) = take(1)

        def keep(*names):
            for i in names:
                pltpu.make_async_copy(kept[i], kept_out[i], kept_sems.at[i]).start()

        if R > d.rows:
            for i in range(t):
                tokbuf[i, d.rows :, :] = jnp.zeros((R - d.rows, D), BF16)
                cot[i, d.rows :, :] = jnp.zeros((R - d.rows, D), BF16)
        tokbuf[z, : d.rows, :] = tok[...]
        cot[z, : d.rows, :] = cot_in[...]
        for i, w in enumerate((wq, wk, wv)):
            w_st[:, i * d.cols : (i + 1) * d.cols] = w[...]
        v_st[...] = jnp.zeros_like(v_st)
        for i, v in enumerate(vecs):
            m = v.shape[0]
            v_st[i : i + 1, :m] = jnp.reshape(v[...].astype(F32), (1, m))
        o_mid[z] = wo[...]
        place.enter()
        l_out.start()
        g_vec.start()
        g_qkv.start()
        l_tok.start()
        at_end = jnp.logical_or(z == 0, z == t - 1)

        @pl.when(at_end)
        def _():
            l_cot.start()

        u_st[...] = jnp.zeros_like(u_st)
        u_st[:, : d.hidden] = wu[...]
        d_st[...] = jnp.zeros_like(d_st)
        d_st[:, : d.hidden] = wd[...]
        bias_part[...] = jnp.zeros_like(bias_part)
        g_vec.forward()
        g_vec.finish()
        for i in range(8):
            vec[i : i + 1, :] = jnp.concatenate([v_all[j, i : i + 1, : d.share] for j in range(n)], axis=1)
        upb[...] = jnp.zeros_like(upb)
        upb[0:1, : d.hidden] = jnp.concatenate(
            [v_all[z * per_line + j, 8:9, : d.up_share] for j in range(per_line)], axis=1
        )
        local = lambda i: jnp.concatenate(
            [v_all[z * per_line + j, i : i + 1, : d.share] for j in range(per_line)], axis=1
        )
        bias_row = jnp.concatenate([local(2), jnp.zeros((1, d.cols), F32), local(3)], axis=1)
        scale_row = jnp.concatenate(
            [jnp.full((1, d.cols), scale_factor, F32), jnp.ones((1, 2 * d.cols), F32)], axis=1
        )
        gain, shift = vec[0:1, :], vec[1:2, :]

        def norm_block(slot):
            def one(r):
                normed = normalize(tokbuf[slot, r, :].astype(F32))[0]
                first[slot, r, :] = (normed * gain + shift).astype(BF16)

            chunks(d, one)

        def project_block(slot):
            y = (dot(first[slot], wqkv[...], NN) + bias_row) * scale_row
            y = y.astype(BF16)
            at = pl.ds(pl.multiple_of(slot * R, R), R)
            for i, ref in enumerate((qh, kh, vh)):
                for j in range(d.heads):
                    start = i * d.cols + j * HD
                    ref[j, at, :] = y[:, start : start + HD]

        norm_block(z)
        l_out.finish()
        o_pack[...] = jnp.concatenate([o_mid[i] for i in range(t)], axis=1)
        g_out.start()
        l_tok.step(1)
        g_qkv.forward()
        g_up.start()
        g_down.start()
        both_sides(place, 1, norm_block)
        g_qkv.finish()
        project_block(z)
        both_sides(place, 1, project_block)

        def norm_and_project(slot):
            norm_block(slot)
            project_block(slot)

        for s in range(2, t):
            l_tok.step(s)

            @pl.when(z == s - 1)
            def _():
                l_cot.relay(0)

            @pl.when(z == t - s)
            def _():
                l_cot.relay(t - 1)

            if s == 2:

                @pl.when(jnp.logical_not(at_end))
                def _():
                    l_cot.start()

            if s == 2:
                g_out.forward()
            both_sides(place, s, norm_and_project)
        g_up.forward()
        keep(0, 1, 2, 5, 6)

        count = jnp.sum(mask[...].astype(F32), axis=1, keepdims=True)
        valid = valid_keys(d, count)
        order = lambda i: jnp.where(lax.rem(i, 2) == 0, lax.div(i, 2), t - 1 - lax.div(i, 2))

        def attend_rows(i, carry):
            r = order(i)
            at = pl.ds(pl.multiple_of(r * R, R), R)

            def head(j, carry):
                scores = dot(qh[j, at, :], kh[j], NT)
                scores = jnp.where(valid > 0, scores, MASK_FILL)
                highest = jnp.max(scores, axis=-1, keepdims=True)
                raised = jnp.exp(scores - highest)
                share = 1.0 / jnp.sum(raised, axis=-1, keepdims=True)
                probs[j, at, :] = (raised * share).astype(BF16)
                mix[j, at, :] = dot(probs[j, at, :], vh[j], NN).astype(BF16)
                return carry

            lax.fori_loop(0, d.heads, head, 0)
            own = [mix[j, at, :] for j in range(d.heads)]
            piece = lambda i, j: own[j][i * d.packed : (i + 1) * d.packed]
            mixbuf[r, z] = jnp.concatenate([piece(i, j) for i in range(t) for j in range(d.heads)], axis=1)
            l_mix(r).start()

            @pl.when(jnp.logical_and(i == 1, jnp.logical_not(at_end)))
            def _():
                for slot in range(1, t - 1):
                    l_cot.relay(slot)

            return carry

        lax.fori_loop(0, t, attend_rows, 0)
        keep(3, 4)
        g_up.finish()
        g_out.finish()
        keep(7)

        def block(i, carry):
            r = order(i)
            l_mix(r).finish()

            rows = jnp.concatenate(
                [
                    jnp.concatenate([mixbuf[r, j, :, k * d.cols : (k + 1) * d.cols] for j in range(t)], axis=1)
                    for k in range(t)
                ],
                axis=0,
            )
            total[...] = tokbuf[r].astype(F32) + dot(rows, out_t[...], NT) + vec[4:5, :]

            @pl.when(r == z)
            def _():
                hidden[...] = total[...]
                mixed_rows[...] = rows

            def norm_two(c):
                normed = normalize(total[c, :])[0]
                second[r, c, :] = (normed * vec[5:6, :] + vec[6:7, :]).astype(BF16)

            chunks(d, norm_two)
            pre = dot(second[r], up[...], NN) + upb[0:1, :]
            value, slope = gelu_both(pre)
            act[r] = value.astype(BF16)

            @pl.when(at_end)
            def _():
                l_cot.relay(r)

            @pl.when(i == 0)
            def _():
                g_down.forward()
                g_down.finish()

            grad = dot(cot[r], down[...], NN) * slope
            bias_part[0:1, :] += jnp.sum(grad, axis=0, keepdims=True)
            pre_grad[r] = grad.astype(BF16)
            part[r] = dot(pre_grad[r], up[...], NT).astype(BF16)

            def launch(these):
                for chain in these:

                    @pl.when(r > 0)
                    def _():
                        chain.launch_right(r)

                    @pl.when(r < t - 1)
                    def _():
                        chain.launch_left(r)

            launch(chains)
            o_part[r] = dot(act[r], down[...], NT).astype(BF16)
            for h in range(1, t - 1):

                @pl.when(i >= h)
                def _():
                    for chain in chains:
                        chain.hop(h, order(i - h))

            return carry

        lax.fori_loop(0, t, block, 0)

        width = D // 3

        def weight_grad(k, left, right, i):
            value = left[:, :, i * width : (i + 1) * width].reshape(d.seq, width)
            grads[k, i * width : (i + 1) * width, :] = dot(value, right[...].reshape(d.seq, HP), TN).astype(BF16)

        work = [partial(weight_grad, 0, second, pre_grad, i) for i in range(3)]
        work += [partial(weight_grad, 1, cot, act, i) for i in range(3)]
        for i in range(t, 2 * t - 2):
            work.pop(0)()
            for h in range(i - t + 1, t - 1):
                for chain in chains:
                    chain.hop(h, order(i - h))
        for item in work:
            item()
        keep(8, 9)
        for (lo, m), chain in zip(split, chains):
            chain.finish(grad_second, pl.ds(lo, m))
        if R > d.sent_rows:
            grad_second[d.sent_rows :, :] = jnp.zeros((R - d.sent_rows, D), F32)
        for op in (l_tok, l_cot):
            op.finish()
        for i in range(10):
            pltpu.make_async_copy(kept[i], kept_out[i], kept_sems.at[i]).wait()

    heads = (d.heads, d.seq, HD)
    outs = [
        shape(16, D, dtype=F32),
        shape(R, D, dtype=F32),
        shape(R, D),
        shape(R, D, dtype=F32),
        shape(8, HP, dtype=F32),
    ]
    kept = [
        shape(*heads),
        shape(*heads),
        shape(*heads),
        shape(*heads),
        shape(d.heads, d.seq, d.seq),
        shape(t, R, D),
        shape(D, 3 * d.cols),
        shape(D, D),
        shape(2, D, HP),
        shape(t, R, D),
    ]
    scratch = [pltpu.VMEM(a.shape, a.dtype) for a in kept]
    scratch += [
        pltpu.VMEM((t, R, D), BF16),
        pltpu.VMEM((d.share, 3 * d.cols), BF16),
        pltpu.VMEM((t, d.share, d.cols), BF16),
        pltpu.VMEM((d.share, D), BF16),
        pltpu.VMEM((d.share, HP), BF16),
        pltpu.VMEM((d.share, HP), BF16),
        pltpu.VMEM((16, d.vec_lanes), F32),
        pltpu.VMEM((n, 16, d.vec_lanes), F32),
        pltpu.VMEM((t, t, d.packed, D), BF16),
        pltpu.VMEM((t, R, D), BF16),
        pltpu.VMEM((t, R, D), BF16),
        pltpu.VMEM((D, HP), BF16),
        pltpu.VMEM((D, HP), BF16),
        pltpu.VMEM((t, R, HP), BF16),
        pltpu.VMEM((t, R, HP), BF16),
        pltpu.VMEM((t, R, D), BF16),
        pltpu.VMEM((t + 1, R, D), BF16),
        pltpu.VMEM((8, HP), F32),
        pltpu.VMEM((R, D), F32),
    ]
    for _ in range(5):
        scratch += DpGather.sems(chips)
    scratch += LineGather.sems(t) + DirectGather.sems(t) + LineGather.sems(t) + DirectGather.sems(t, (t,))
    scratch += LineChain.sems(t) * 2 + [DMA((10,))]
    return pl.pallas_call(
        kernel,
        out_shape=outs + kept,
        in_specs=[VM] * len(args),
        out_specs=[VM] * len(outs) + [ANY] * len(kept),
        scratch_shapes=scratch,
        compiler_params=params(0),
        name="forward",
    )(*args)


class DpAdd:
    @staticmethod
    def sems(chips):
        return [DMA((chips,)), DMA((chips,)), DMA((chips,)), DMA((chips,))]

    def __init__(self, place, part, rows, near, far, sems):
        self.p, self.part, self.rows, self.near, self.far = place, part, rows, near, far
        self.sent, self.recv, self.sent_far, self.recv_far = sems

    def at(self, slot):
        return pl.ds(pl.multiple_of(slot * self.rows, 8), self.rows)

    def start(self):
        p = self.p
        for k in [*range(1, p.chips), 0]:
            src = self.part.at[self.at(2 * p.chip_at(k) + 1 - p.core)]
            remote(src, self.near.at[k], self.sent.at[k], self.recv.at[k], p.sibling).start()

    def wait_near(self, k):
        block = self.near.at[k]
        remote(block, block, self.sent.at[k], self.recv.at[k], self.p.sibling).wait_recv()

    def move(self):
        p = self.p
        for k in range(1, p.chips):
            self.wait_near(k)
            mine = self.part[self.at(2 * p.chip_at(k) + p.core), :]
            self.near[k] = (mine.astype(F32) + self.near[k].astype(F32)).astype(BF16)
            remote(self.near.at[k], self.far.at[k - 1], self.sent_far.at[k], self.recv_far.at[k], p.peer(k)).start()

    def finish(self):
        p = self.p
        self.wait_near(0)
        total = self.part[self.at(p.dp), :].astype(F32) + self.near[0].astype(F32)
        for k in range(1, p.chips):
            block = self.far.at[k - 1]
            remote(block, block, self.sent_far.at[k], self.recv_far.at[k], p.sibling).wait_recv()
            total += self.far[k - 1].astype(F32)
        for k in range(p.chips):
            block = self.near.at[0]
            remote(block, block, self.sent.at[k], self.recv.at[0], p.sibling).wait_send()
            if k > 0:
                remote(block, block, self.sent_far.at[k], self.recv.at[0], p.sibling).wait_send()
        return total


def backward(d, args):
    n, t, R, D, HP = d.n, d.t, d.block, d.width, d.hidden_pad
    chips, per_line, share = n // 2, n // t, d.share
    scale_factor = 1.0 / math.sqrt(HD)
    wide = 3 * d.cols

    def kernel(*refs):
        refs = list(refs)
        take = lambda m: [refs.pop(0) for _ in range(m)]
        tok, cot, hidden, grad_second, vec, mixed_rows, bias_part = take(7)
        far = take(10)
        output, input_grad, g_qkv, g_out, g_up, g_down, g_vec = take(7)
        near = take(10)
        qh, kh, vh, mix, probs, first, wqkv, out_t, grads_mlp, p_part = near
        tok_p, cot_p, gh, low, send, got, dq, dk, dv, q_sum, grads = take(11)
        o_part, w_part, f_part, f_inbox, p_inbox, f_sum, acc = take(7)
        o_mid, o_got, v_send, v_got, v_mid, v_line = take(6)
        place = Place(n, t)
        z, dp = place.z, place.dp

        def adder(part):
            near, far = take(2)
            return part, near, far

        up_grad, down_grad = grads_mlp.at[0], grads_mlp.at[1]
        spaces = [adder(part) for part in (up_grad, down_grad, o_part, w_part)]
        sum_up, sum_down, sum_out, sum_qkv = [
            DpAdd(place, part, share, near, far, take(4)) for part, near, far in spaces
        ]
        split = halves(d)
        view = lambda ref, lo, m: ref.at[:, pl.ds(lo, m)]
        f_chains = [LineChain(place, view(f_part, *h), view(f_inbox, *h), take(2)) for h in split]
        p_chains = [LineChain(place, view(p_part, *h), view(p_inbox, *h), take(2)) for h in split]
        exchange = LineExchange(place, o_mid, o_got, take(3))
        x_sent, x_recv, v_sent, v_recv, v_sent_line, v_recv_line, far_sems = take(7)
        load = lambda i: pltpu.make_async_copy(far[i], near[i], far_sems.at[i])
        for i in (7, 9, 8, 4, 0, 1, 2, 3, 6, 5):
            load(i).start()
        place.enter(every=True)
        for ref, src in ((tok_p, tok), (cot_p, cot)):
            ref[: d.rows, :] = src[...]
            if R > d.rows:
                ref[d.rows :, :] = jnp.zeros((R - d.rows, D), BF16)
        acc[...] = jnp.zeros_like(acc)

        def add_row(i, value):
            acc[i : i + 1, :] += jnp.sum(value, axis=0, keepdims=True)

        def norm_two(r):
            normed, inv = normalize(hidden[r, :])
            grad = grad_second[r, :]
            scaled = grad * vec[5:6, :]
            cots = cot_p[r, :].astype(F32)
            mean = jnp.mean(scaled, axis=-1, keepdims=True)
            pull = jnp.mean(scaled * normed, axis=-1, keepdims=True)
            total = cots + inv * (scaled - mean - normed * pull)
            gh[r, :] = total
            low[r, :] = total.astype(BF16)
            add_row(5, grad * normed)
            add_row(6, grad)
            add_row(4, total)
            add_row(7, cots)

        chunks(d, norm_two)
        load(7).wait()
        mixed_grad = dot(low[...], out_t[...], NN).astype(BF16)
        for i in range(t):
            own = mixed_grad[:, i * d.cols : (i + 1) * d.cols]
            send[i] = jnp.concatenate([own[j * d.packed : (j + 1) * d.packed] for j in range(t)], axis=1)
        for k in range(1, t):
            to = place.along(k)
            remote(send.at[to[1]], got.at[z], x_sent.at[k], x_recv.at[z], to).start()
        got[z] = send[z]
        load(9).wait()
        for i in range(t - 1, 0, -1):
            for chain in p_chains:
                chain.launch_right(i)
                chain.launch_left(t - 1 - i)
        load(8).wait()
        sum_up.start()
        sum_down.start()
        third = D // 3
        for i in range(3):
            o_part[i * third : (i + 1) * third, :] = dot(
                low[:, i * third : (i + 1) * third], mixed_rows[...], TN
            ).astype(BF16)
        sum_out.start()
        for i in range(5):
            load(i).wait()

        for ref in (dk, dv, q_sum):
            ref[...] = jnp.zeros_like(ref)

        def attend_rows(r):
            at = pl.ds(pl.multiple_of(r * R, R), R)
            for j in range(d.heads):
                pieces = [got[r, :, i * d.cols + j * HD : i * d.cols + (j + 1) * HD] for i in range(t)]
                dq[j, at, :] = jnp.concatenate(pieces, axis=0)

            def head(j, carry):
                grad = dq[j, at, :]
                full = probs[j, at, :]
                dv[j] += dot(full, grad, TN)
                delta = jnp.sum(grad.astype(F32) * mix[j, at, :].astype(F32), axis=-1, keepdims=True)
                grad_scores = (full.astype(F32) * (dot(grad, vh[j], NT) - delta)).astype(BF16)
                dk[j] += dot(grad_scores, qh[j, at, :], TN)
                query = dot(grad_scores, kh[j], NN) * scale_factor
                q_sum[j, 0:1, :] += jnp.sum(query, axis=0, keepdims=True)
                dq[j, at, :] = query.astype(BF16)
                return carry

            lax.fori_loop(0, d.heads, head, 0)

        attend_rows(z)
        sum_up.move()
        for k in range(1, t):
            slot = place.along(k)[1]
            remote(got.at[slot], got.at[slot], x_sent.at[k], x_recv.at[slot], place.sibling).wait_recv()
            attend_rows(slot)
            if k == 1:
                sum_down.move()
            if k == 2:
                sum_out.move()
        load(6).wait()
        load(5).wait()

        def part_block(i):
            slot = jnp.where(z < t // 2, t - 1 - i, i)
            at = pl.ds(pl.multiple_of(slot * R, R), R)
            values = [dq[j, at, :] for j in range(d.heads)]
            values += [ref[j, at, :].astype(BF16) for ref in (dk, dv) for j in range(d.heads)]
            grads[at, :] = jnp.concatenate(values, axis=1)
            f_part[slot] = dot(grads[at, :], wqkv[...], NT).astype(BF16)
            for chain in f_chains:

                @pl.when(slot > 0)
                def _():
                    chain.launch_right(slot)

                @pl.when(slot < t - 1)
                def _():
                    chain.launch_left(slot)

        for i in range(1, t - 1):
            for chain in p_chains:
                chain.tick_far(i)
        for i in range(t):
            part_block(i)

        def weight_block(i):
            value = first[:, :, i * third : (i + 1) * third].reshape(d.seq, third)
            w_part[i * third : (i + 1) * third, :] = dot(value, grads[...], TN).astype(BF16)

        for i in range(3):
            weight_block(i)
        sum_qkv.start()
        for i in range(1, t - 1):
            for chain in f_chains:
                chain.tick_far(i)
        for (lo, m), chain in zip(split, p_chains):
            chain.finish(f_sum, pl.ds(lo, m))
        if R > d.sent_rows:
            f_sum[d.sent_rows :, :] = jnp.zeros((R - d.sent_rows, D), F32)
        output[...] = (hidden[...] + f_sum[...] + vec[7:8, :]).astype(BF16)
        g_up[...] = sum_up.finish()
        sum_qkv.move()
        g_down[...] = sum_down.finish()
        out_total = sum_out.finish().astype(BF16)
        for i in range(t):
            o_mid[i] = out_total[:, i * d.cols : (i + 1) * d.cols]
        exchange.start()
        for (lo, m), chain in zip(split, f_chains):
            chain.finish(f_sum, pl.ds(lo, m))
        if R > d.sent_rows:
            f_sum[d.sent_rows :, :] = jnp.zeros((R - d.sent_rows, D), F32)

        def norm_one(r):
            normed, inv = normalize(tok_p[r, :].astype(F32))
            grad = f_sum[r, :]
            scaled = grad * vec[0:1, :]
            mean = jnp.mean(scaled, axis=-1, keepdims=True)
            pull = jnp.mean(scaled * normed, axis=-1, keepdims=True)
            input_grad[r, :] = gh[r, :] + inv * (scaled - mean - normed * pull)
            add_row(0, grad * normed)
            add_row(1, grad)

        chunks(d, norm_one)
        v_send[...] = jnp.zeros_like(v_send)
        for i in (0, 1, 4, 5, 6, 7):
            for j in range(n):
                v_send[j, i : i + 1, :share] = acc[i : i + 1, j * share : (j + 1) * share]
        q_row = jnp.concatenate([q_sum[j, 0:1, :] for j in range(d.heads)], axis=1)
        v_row = jnp.concatenate([jnp.sum(dv[j], axis=0, keepdims=True) for j in range(d.heads)], axis=1)
        for j in range(per_line):
            slot = z * per_line + j
            v_send[slot, 2:3, :share] = q_row[:, j * share : (j + 1) * share]
            v_send[slot, 3:4, :share] = v_row[:, j * share : (j + 1) * share]
            v_send[slot, 8:9, : d.up_share] = bias_part[0:1, j * d.up_share : (j + 1) * d.up_share]
        others = [lax.rem(dp + k, n) for k in range(1, n)]
        for k in range(1, n):
            to = others[k - 1]
            remote(v_send.at[to], v_got.at[k], v_sent.at[k], v_recv.at[k], (to, z)).start()
        g_qkv[...] = sum_qkv.finish()
        total = v_send[dp]
        for k in range(1, n):
            remote(v_got.at[k], v_got.at[k], v_sent.at[k], v_recv.at[k], place.sibling).wait()
            total += v_got[k]
        v_mid[...] = total
        for k in range(1, t):
            remote(v_mid, v_line.at[k], v_sent_line.at[k], v_recv_line.at[k], place.along(k)).start()
        exchange.finish()
        g_out[...] = jnp.sum(o_got[...].astype(F32), axis=0)
        for k in range(1, t):
            remote(v_mid, v_line.at[k], v_sent_line.at[k], v_recv_line.at[k], place.sibling).wait()
            total += v_line[k]
        g_vec[...] = total
        for k in range(1, t):
            remote(send.at[0], got.at[0], x_sent.at[k], x_recv.at[0], place.sibling).wait_send()

    outs = [
        shape(R, D),
        shape(R, D, dtype=F32),
        shape(share, wide, dtype=F32),
        shape(share, d.cols, dtype=F32),
        shape(share, HP, dtype=F32),
        shape(share, HP, dtype=F32),
        shape(16, d.vec_lanes, dtype=F32),
    ]
    heads = (d.heads, d.seq, HD)
    scratch = [pltpu.VMEM(a.shape, a.dtype) for a in args[7:]]
    scratch += [
        pltpu.VMEM((R, D), BF16),
        pltpu.VMEM((R, D), BF16),
        pltpu.VMEM((R, D), F32),
        pltpu.VMEM((R, D), BF16),
        pltpu.VMEM((t, d.packed, D), BF16),
        pltpu.VMEM((t, d.packed, D), BF16),
        pltpu.VMEM(heads, BF16),
        pltpu.VMEM(heads, F32),
        pltpu.VMEM(heads, F32),
        pltpu.VMEM((d.heads, 8, HD), F32),
        pltpu.VMEM((d.seq, wide), BF16),
        pltpu.VMEM((D, D), BF16),
        pltpu.VMEM((D, wide), BF16),
        pltpu.VMEM((t, R, D), BF16),
        pltpu.VMEM((t + 1, R, D), BF16),
        pltpu.VMEM((t + 1, R, D), BF16),
        pltpu.VMEM((R, D), F32),
        pltpu.VMEM((16, D), F32),
        pltpu.VMEM((t, share, d.cols), BF16),
        pltpu.VMEM((t, share, d.cols), BF16),
        pltpu.VMEM((n, 16, d.vec_lanes), F32),
        pltpu.VMEM((n, 16, d.vec_lanes), F32),
        pltpu.VMEM((16, d.vec_lanes), F32),
        pltpu.VMEM((t, 16, d.vec_lanes), F32),
    ]
    for width in (HP, HP, D, wide):
        scratch += [pltpu.VMEM((chips, share, width), BF16), pltpu.VMEM((chips - 1, share, width), BF16)]
    scratch += DpAdd.sems(chips) * 4 + LineChain.sems(t) * 4 + LineExchange.sems(t)
    scratch += [DMA((t,)), DMA((t,)), DMA((n,)), DMA((n,)), DMA((t,)), DMA((t,)), DMA((10,))]
    return pl.pallas_call(
        kernel,
        out_shape=outs,
        in_specs=[VM] * 7 + [ANY] * 10,
        out_specs=[VM] * len(outs),
        scratch_shapes=scratch,
        compiler_params=params(1),
        name="backward",
    )(*args)


def finalize(d, args):
    rows, share, cols = d.rows, d.share, d.cols

    def kernel(out_p, grad_p, g_qkv, g_out, g_up, g_down, g_vec, *outs):
        output, input_grad, q, k, v, o, up, down = outs[:8]
        output[...] = out_p[:rows, :]
        input_grad[...] = grad_p[:rows, :]
        for i, ref in enumerate((q, k, v)):
            ref[...] = g_qkv[:, i * cols : (i + 1) * cols]
        o[...] = g_out[...]
        up[...] = g_up[:, : d.hidden]
        down[...] = g_down[:, : d.hidden]
        for i, ref in enumerate(outs[8:]):
            m = ref.shape[0]
            ref[...] = jnp.reshape(g_vec[i : i + 1, :m], (m,))

    f32 = partial(shape, dtype=F32)
    outs = [shape(rows, d.width), f32(rows, d.width)] + [f32(share, cols)] * 3
    outs += [f32(share, cols), f32(share, d.hidden), f32(share, d.hidden)] + [f32(share)] * 8 + [f32(d.up_share)]
    return pl.pallas_call(
        kernel,
        out_shape=outs,
        in_specs=[VM] * len(args),
        out_specs=[VM] * len(outs),
        compiler_params=pltpu.CompilerParams(vmem_limit_bytes=VMEM_BYTES),
        name="finalize",
    )(*args)


def shards(
    sizes,
    tokens,
    key_mask,
    query_weight,
    key_weight,
    value_weight,
    out_weight,
    up_weight,
    down_weight,
    first_gain,
    first_shift,
    query_bias,
    value_bias,
    out_bias,
    second_gain,
    second_shift,
    up_bias,
    down_bias,
    cotangent,
):
    rows, width = tokens.shape[1:]
    share, up_share = first_gain.shape[0], up_bias.shape[0]
    cols, hidden_cols = query_weight.shape[1], up_weight.shape[1]
    d = Dims(sizes, rows, width, share, cols, hidden_cols, up_share)
    small = [first_gain, first_shift, query_bias, value_bias, out_bias, second_gain, second_shift, down_bias]
    vec, hidden, mixed_rows, grad_second, bias_part, *kept = forward(
        d,
        [tokens[0], cotangent[0], key_mask, query_weight, key_weight, value_weight, out_weight.T, up_weight, down_weight.T]
        + small
        + [up_bias],
    )
    parts = backward(d, [tokens[0], cotangent[0], hidden, grad_second, vec, mixed_rows, bias_part, *kept])
    outs = finalize(d, parts)
    vectors = outs[8:]
    return (outs[0][None], outs[1][None], *outs[2:5], outs[5].T, outs[6], outs[7].T, *vectors[:7], vectors[8], vectors[7])


def solution(mesh):
    sizes = (mesh.shape["dp"], mesh.shape["tensor"])
    split = P("dp", "tensor")
    return jax.shard_map(
        partial(shards, sizes),
        mesh=mesh,
        in_specs=(P("dp", "tensor", None), P("dp", None), split, split, split, P("tensor", "dp"), split, P("tensor", "dp"))
        + (P("dp"),) * 9
        + (P("dp", "tensor", None),),
        out_specs=(P("dp", "tensor", None), P("dp", "tensor", None), split, split, split, P("tensor", "dp"), split, P("tensor", "dp"))
        + (P("dp"),) * 9,
        check_vma=False,
    )
```

time: 754 us -> 228 us (0.30)
  waiting for transfers between devices: 490 us -> 0 us
  Pallas kernels: 0 us -> 227 us
  blocking collectives: 110 us -> 0 us
  matrix products: 86 us -> 0 us
  other arithmetic: 22.3 us -> 0 us
  local copies, waits for them, and re-layouts: 20.8 us -> 0 us
  between operations: 17.6 us -> 0.86 us
    reduce_scatter x6 -> x0, waiting for transfers between devices: 243 us -> none  [the longest x1 61.1 us: shards(): lax.psum_scatter(up_grad, 'dp', scatter_dimension=0, tiled=True)]
    pallas_call x0 -> x3, Pallas kernels: none -> 227 us  [the longest x1 129 us: forward(): pl.pallas_call(kernel, out_shape=outs + kept, in_specs=[VM] * len(args),...]
    all_gather x6 -> x0, waiting for transfers between devices: 139 us -> none  [the longest x4 108 us: gather_rows(): return lax.all_gather(local, 'tensor', axis=1, tiled=True)]
    unnamed x20 -> x0, waiting for transfers between devices: 109 us -> none
    dot_general x24 -> x0, matrix products: 86 us -> none  [the longest x18 68.8 us: mat_dot(): return jnp.dot(left, right, preferred_element_type=jnp.float32)]
    all_gather x4 -> x0, blocking collectives: 42.4 us -> none  [the longest x1 11.8 us: shards(): lax.all_gather(out_weight, 'dp', axis=1, tiled=True)]
    psum x1 -> x0, blocking collectives: 41.8 us -> none  [shards(): lax.psum((first_gain_grad, first_shift_grad, query_bias_full, value_bias_...]
    unnamed x1 -> x0, blocking collectives: 26.1 us -> none
  transfers between devices with their start and end apart: 16 -> 0, of which waited for: 14 -> 0; matrix products, arithmetic and copies ran while one was open for 8% -> 0% of each run, Pallas kernels for 0% -> 0%
where the time goes in v2:
time: 228 us
  Pallas kernels  227 us (100%)
    pallas_call x1, Pallas kernels, forward(): pl.pallas_call(kernel, out_shape=outs + kept, in_specs=[VM] * len(args),...  129 us
    pallas_call x1, Pallas kernels, backward(): pl.pallas_call(kernel, out_shape=outs, in_specs=[VM] * 7 + [ANY] * 10, ou...  93.8 us

profile of v2, /device:TPU:0, one launch (start us, length us, event | category | flops | bytes accessed | tf_op | source)
XLA Modules:
  0.0 227.7 jit_solution(10167175930904613323)
XLA Ops:
  0.7 129.3 %forward.1 = (f32[16,1152]{1,0:T(8,128)}, f32[192,1152]{1,0:T(8,128)}, bf16[192,1152]{1,0:T(8,128)(2,1)}, f32[192,1152]{1,0:T(8,128)}, f32[8,1152]{1,0:T(8,128)}...) custom-call(bf16[184,1152]{1,0:T(8,128)(2,1)} %bitcast.8, ...), custom_call_target="tpu_custom_call" | custom-call | tf_op jit(solution)/shard_map/forward/pallas_call | solution.py:710
  130.0 93.8 %backward.1 = (bf16[192,1152]{1,0:T(8,128)(2,1)}, f32[192,1152]{1,0:T(8,128)}, f32[144,864]{1,0:T(8,128)}, f32[144,288]{1,0:T(8,128)}, f32[144,1152]{1,0:T(8,128...) custom-call(bf16[184,1152]{1,0:T(8,128)(2,1)} %bitcast.9, bf16[184,1152]{1,0:T(8,128)(2,1)} %bitcast.11, ...), custom_call_target="tpu_custom_call" | custom-call | tf_op jit(solution)/shard_map/backward/pallas_call | solution.py:1027
  223.7 3.8 %finalize.1 = (bf16[184,1152]{1,0:T(8,128)(2,1)}, f32[184,1152]{1,0:T(8,128)}, f32[144,288]{1,0:T(8,128)}, f32[144,288]{1,0:T(8,128)}, f32[144,288]{1,0:T(8,128)...) custom-call(bf16[192,1152]{1,0:T(8,128)(2,1)} %get-tuple-element.71., ...), custom_call_target="tpu_custom_call" | custom-call | tf_op jit(solution)/shard_map/finalize/pallas_call | solution.py:1057

commit v3 on v2

--- a/solution.py
+++ b/solution.py
@@ -50,18 +50,19 @@
     def along(self, k):
         return (self.dp, lax.rem(self.z + k + self.line, self.line))
 
-    def enter(self, across=True, line=True, every=False):
+    def greet(self, every=False):
         barrier = pltpu.get_barrier_semaphore()
-        devices = []
         if every:
-            devices += [(lax.rem(self.dp + k, self.dp_size), self.z) for k in range(1, self.dp_size)]
-        elif across:
-            devices += [self.peer(k) for k in range(1, self.chips)] + [self.sibling]
-        if line:
-            devices += [self.along(k) for k in range(1, self.line)]
+            devices = [(lax.rem(self.dp + k, self.dp_size), self.z) for k in range(1, self.dp_size)]
+        else:
+            devices = [self.peer(k) for k in range(1, self.chips)] + [self.sibling]
+        devices += [self.along(k) for k in range(1, self.line)]
         for device in devices:
             pl.semaphore_signal(barrier, inc=1, device_id=device, device_id_type=MESH)
-        pl.semaphore_wait(barrier, len(devices))
+        self.partners = len(devices)
+
+    def meet(self):
+        pl.semaphore_wait(pltpu.get_barrier_semaphore(), self.partners)
 
 
 class DpGather:
@@ -259,6 +260,8 @@
         self.hidden_pad = pad_to(hidden, 128)
         self.vec_lanes = pad_to(max(up_share, share), 128)
         self.packed = self.block // self.t
+        self.folds = 3 if share % 3 == 0 else 1
+        self.fold = share // self.folds
         self.chunk = 32 if self.block % 32 == 0 else 16
 
 
@@ -412,6 +415,7 @@
         tokbuf, w_st, o_mid, o_pack, u_st, d_st, v_st, v_all = take(8)
         mixbuf, second, cot, up, down, act, pre_grad, part, inbox, upb, total = take(11)
         place = Place(n, t)
+        place.greet()
         z = place.z
         rows_of = lambda ref: (lambda slot: ref.at[pl.ds(pl.multiple_of(slot * d.share, 8), d.share)])
         g_vec = DpGather(place, v_st, v_all, take(4))
@@ -444,8 +448,8 @@
         for i, v in enumerate(vecs):
             m = v.shape[0]
             v_st[i : i + 1, :m] = jnp.reshape(v[...].astype(F32), (1, m))
-        o_mid[z] = wo[...]
-        place.enter()
+        o_mid[z] = jnp.concatenate([wo[i * d.fold : (i + 1) * d.fold, :] for i in range(d.folds)], axis=1)
+        place.meet()
         l_out.start()
         g_vec.start()
         g_qkv.start()
@@ -496,7 +500,10 @@
 
         norm_block(z)
         l_out.finish()
-        o_pack[...] = jnp.concatenate([o_mid[i] for i in range(t)], axis=1)
+        for i in range(d.folds):
+            o_pack[i * d.fold : (i + 1) * d.fold, :] = jnp.concatenate(
+                [o_mid[j, :, i * d.cols : (i + 1) * d.cols] for j in range(t)], axis=1
+            )
         g_out.start()
         l_tok.step(1)
         g_qkv.forward()
@@ -536,7 +543,11 @@
 
         count = jnp.sum(mask[...].astype(F32), axis=1, keepdims=True)
         valid = valid_keys(d, count)
-        order = lambda i: jnp.where(lax.rem(i, 2) == 0, lax.div(i, 2), t - 1 - lax.div(i, 2))
+
+
+        def order(i):
+            pair = lax.div(i, 2)
+            return jnp.where(lax.rem(i + pair, 2) == 0, pair, t - 1 - pair)
 
         def attend_rows(i, carry):
             r = order(i)
@@ -558,11 +569,6 @@
             mixbuf[r, z] = jnp.concatenate([piece(i, j) for i in range(t) for j in range(d.heads)], axis=1)
             l_mix(r).start()
 
-            @pl.when(jnp.logical_and(i == 1, jnp.logical_not(at_end)))
-            def _():
-                for slot in range(1, t - 1):
-                    l_cot.relay(slot)
-
             return carry
 
         lax.fori_loop(0, t, attend_rows, 0)
@@ -574,6 +580,11 @@
         def block(i, carry):
             r = order(i)
             l_mix(r).finish()
+
+            @pl.when(jnp.logical_and(i == 2, jnp.logical_not(at_end)))
+            def _():
+                for slot in range(1, t - 1):
+                    l_cot.relay(slot)
 
             rows = jnp.concatenate(
                 [
@@ -685,7 +696,7 @@
     scratch += [
         pltpu.VMEM((t, R, D), BF16),
         pltpu.VMEM((d.share, 3 * d.cols), BF16),
-        pltpu.VMEM((t, d.share, d.cols), BF16),
+        pltpu.VMEM((t, d.fold, d.folds * d.cols), BF16),
         pltpu.VMEM((d.share, D), BF16),
         pltpu.VMEM((d.share, HP), BF16),
         pltpu.VMEM((d.share, HP), BF16),
@@ -775,13 +786,14 @@
         take = lambda m: [refs.pop(0) for _ in range(m)]
         tok, cot, hidden, grad_second, vec, mixed_rows, bias_part = take(7)
         far = take(10)
-        output, input_grad, g_qkv, g_out, g_up, g_down, g_vec = take(7)
+        output, input_grad, g_q, g_k, g_v, g_out, g_up, g_down, g_vec = take(9)
         near = take(10)
         qh, kh, vh, mix, probs, first, wqkv, out_t, grads_mlp, p_part = near
         tok_p, cot_p, gh, low, send, got, dq, dk, dv, q_sum, grads = take(11)
         o_part, w_part, f_part, f_inbox, p_inbox, f_sum, acc = take(7)
         o_mid, o_got, v_send, v_got, v_mid, v_line = take(6)
         place = Place(n, t)
+        place.greet(every=True)
         z, dp = place.z, place.dp
 
         def adder(part):
@@ -800,9 +812,16 @@
         exchange = LineExchange(place, o_mid, o_got, take(3))
         x_sent, x_recv, v_sent, v_recv, v_sent_line, v_recv_line, far_sems = take(7)
         load = lambda i: pltpu.make_async_copy(far[i], near[i], far_sems.at[i])
-        for i in (7, 9, 8, 4, 0, 1, 2, 3, 6, 5):
+        for i in (9, 8, 7, 4, 0, 1, 2, 3, 6, 5):
             load(i).start()
-        place.enter(every=True)
+        place.meet()
+        load(9).wait()
+        for chain in p_chains:
+            chain.launch_right(t - 1)
+            chain.launch_left(0)
+        load(8).wait()
+        sum_up.start()
+        sum_down.start()
         for ref, src in ((tok_p, tok), (cot_p, cot)):
             ref[: d.rows, :] = src[...]
             if R > d.rows:
@@ -837,14 +856,13 @@
             to = place.along(k)
             remote(send.at[to[1]], got.at[z], x_sent.at[k], x_recv.at[z], to).start()
         got[z] = send[z]
-        load(9).wait()
-        for i in range(t - 1, 0, -1):
+        for i in range(t - 2, 1, -1):
             for chain in p_chains:
                 chain.launch_right(i)
                 chain.launch_left(t - 1 - i)
-        load(8).wait()
-        sum_up.start()
-        sum_down.start()
+        p_chains[0].launch_right(1)
+        p_chains[0].launch_left(t - 2)
+        sum_up.move()
         third = D // 3
         for i in range(3):
             o_part[i * third : (i + 1) * third, :] = dot(
@@ -878,15 +896,15 @@
             lax.fori_loop(0, d.heads, head, 0)
 
         attend_rows(z)
-        sum_up.move()
+        sum_down.move()
         for k in range(1, t):
             slot = place.along(k)[1]
             remote(got.at[slot], got.at[slot], x_sent.at[k], x_recv.at[slot], place.sibling).wait_recv()
             attend_rows(slot)
             if k == 1:
-                sum_down.move()
-            if k == 2:
                 sum_out.move()
+                for chain in p_chains:
+                    chain.tick_far(1)
         load(6).wait()
         load(5).wait()
 
@@ -907,11 +925,14 @@
                 def _():
                     chain.launch_left(slot)
 
-        for i in range(1, t - 1):
+        for i in range(t):
+            part_block(i)
+        for chain in p_chains[1:]:
+            chain.launch_right(1)
+            chain.launch_left(t - 2)
+        for i in range(2, t - 1):
             for chain in p_chains:
                 chain.tick_far(i)
-        for i in range(t):
-            part_block(i)
 
         def weight_block(i):
             value = first[:, :, i * third : (i + 1) * third].reshape(d.seq, third)
@@ -920,41 +941,21 @@
         for i in range(3):
             weight_block(i)
         sum_qkv.start()
-        for i in range(1, t - 1):
+        g_up[...] = sum_up.finish()[:, : d.hidden]
+        for chain in f_chains:
+            chain.tick_far(1)
+        sum_qkv.move()
+        g_down[...] = sum_down.finish()[:, : d.hidden]
+        for i in range(2, t - 1):
             for chain in f_chains:
                 chain.tick_far(i)
-        for (lo, m), chain in zip(split, p_chains):
-            chain.finish(f_sum, pl.ds(lo, m))
-        if R > d.sent_rows:
-            f_sum[d.sent_rows :, :] = jnp.zeros((R - d.sent_rows, D), F32)
-        output[...] = (hidden[...] + f_sum[...] + vec[7:8, :]).astype(BF16)
-        g_up[...] = sum_up.finish()
-        sum_qkv.move()
-        g_down[...] = sum_down.finish()
         out_total = sum_out.finish().astype(BF16)
         for i in range(t):
-            o_mid[i] = out_total[:, i * d.cols : (i + 1) * d.cols]
+            o_mid[i] = jnp.concatenate(
+                [out_total[j * d.fold : (j + 1) * d.fold, i * d.cols : (i + 1) * d.cols] for j in range(d.folds)], axis=1
+            )
         exchange.start()
-        for (lo, m), chain in zip(split, f_chains):
-            chain.finish(f_sum, pl.ds(lo, m))
-        if R > d.sent_rows:
-            f_sum[d.sent_rows :, :] = jnp.zeros((R - d.sent_rows, D), F32)
-
-        def norm_one(r):
-            normed, inv = normalize(tok_p[r, :].astype(F32))
-            grad = f_sum[r, :]
-            scaled = grad * vec[0:1, :]
-            mean = jnp.mean(scaled, axis=-1, keepdims=True)
-            pull = jnp.mean(scaled * normed, axis=-1, keepdims=True)
-            input_grad[r, :] = gh[r, :] + inv * (scaled - mean - normed * pull)
-            add_row(0, grad * normed)
-            add_row(1, grad)
-
-        chunks(d, norm_one)
         v_send[...] = jnp.zeros_like(v_send)
-        for i in (0, 1, 4, 5, 6, 7):
-            for j in range(n):
-                v_send[j, i : i + 1, :share] = acc[i : i + 1, j * share : (j + 1) * share]
         q_row = jnp.concatenate([q_sum[j, 0:1, :] for j in range(d.heads)], axis=1)
         v_row = jnp.concatenate([jnp.sum(dv[j], axis=0, keepdims=True) for j in range(d.heads)], axis=1)
         for j in range(per_line):
@@ -962,11 +963,33 @@
             v_send[slot, 2:3, :share] = q_row[:, j * share : (j + 1) * share]
             v_send[slot, 3:4, :share] = v_row[:, j * share : (j + 1) * share]
             v_send[slot, 8:9, : d.up_share] = bias_part[0:1, j * d.up_share : (j + 1) * d.up_share]
+        for (lo, m), chain in zip(split, f_chains):
+            chain.finish(f_sum, pl.ds(lo, m))
+        if R > d.sent_rows:
+            f_sum[d.sent_rows :, :] = jnp.zeros((R - d.sent_rows, D), F32)
+
+        def norm_one_sums(r):
+            normed = normalize(tok_p[r, :].astype(F32))[0]
+            grad = f_sum[r, :]
+            add_row(0, grad * normed)
+            add_row(1, grad)
+
+        def norm_one(r):
+            normed, inv = normalize(tok_p[r, :].astype(F32))
+            scaled = f_sum[r, :] * vec[0:1, :]
+            mean = jnp.mean(scaled, axis=-1, keepdims=True)
+            pull = jnp.mean(scaled * normed, axis=-1, keepdims=True)
+            input_grad[r, :] = gh[r, :] + inv * (scaled - mean - normed * pull)
+
+        chunks(d, norm_one_sums)
+        for i in (0, 1, 4, 5, 6, 7):
+            for j in range(n):
+                v_send[j, i : i + 1, :share] = acc[i : i + 1, j * share : (j + 1) * share]
         others = [lax.rem(dp + k, n) for k in range(1, n)]
         for k in range(1, n):
             to = others[k - 1]
             remote(v_send.at[to], v_got.at[k], v_sent.at[k], v_recv.at[k], (to, z)).start()
-        g_qkv[...] = sum_qkv.finish()
+        chunks(d, norm_one)
         total = v_send[dp]
         for k in range(1, n):
             remote(v_got.at[k], v_got.at[k], v_sent.at[k], v_recv.at[k], place.sibling).wait()
@@ -974,8 +997,18 @@
         v_mid[...] = total
         for k in range(1, t):
             remote(v_mid, v_line.at[k], v_sent_line.at[k], v_recv_line.at[k], place.along(k)).start()
+        qkv_total = sum_qkv.finish()
+        for i, ref in enumerate((g_q, g_k, g_v)):
+            ref[...] = qkv_total[:, i * d.cols : (i + 1) * d.cols]
         exchange.finish()
-        g_out[...] = jnp.sum(o_got[...].astype(F32), axis=0)
+        out_sum = jnp.sum(o_got[...].astype(F32), axis=0)
+        for i in range(d.folds):
+            g_out[i * d.fold : (i + 1) * d.fold, :] = out_sum[:, i * d.cols : (i + 1) * d.cols]
+        for (lo, m), chain in zip(split, p_chains):
+            chain.finish(f_sum, pl.ds(lo, m))
+        if R > d.sent_rows:
+            f_sum[d.sent_rows :, :] = jnp.zeros((R - d.sent_rows, D), F32)
+        output[...] = (hidden[...] + f_sum[...] + vec[7:8, :]).astype(BF16)
         for k in range(1, t):
             remote(v_mid, v_line.at[k], v_sent_line.at[k], v_recv_line.at[k], place.sibling).wait()
             total += v_line[k]
@@ -986,10 +1019,12 @@
     outs = [
         shape(R, D),
         shape(R, D, dtype=F32),
-        shape(share, wide, dtype=F32),
         shape(share, d.cols, dtype=F32),
-        shape(share, HP, dtype=F32),
-        shape(share, HP, dtype=F32),
+        shape(share, d.cols, dtype=F32),
+        shape(share, d.cols, dtype=F32),
+        shape(share, d.cols, dtype=F32),
+        shape(share, d.hidden, dtype=F32),
+        shape(share, d.hidden, dtype=F32),
         shape(16, d.vec_lanes, dtype=F32),
     ]
     heads = (d.heads, d.seq, HD)
@@ -1013,8 +1048,8 @@
         pltpu.VMEM((t + 1, R, D), BF16),
         pltpu.VMEM((R, D), F32),
         pltpu.VMEM((16, D), F32),
-        pltpu.VMEM((t, share, d.cols), BF16),
-        pltpu.VMEM((t, share, d.cols), BF16),
+        pltpu.VMEM((t, d.fold, d.folds * d.cols), BF16),
+        pltpu.VMEM((t, d.fold, d.folds * d.cols), BF16),
         pltpu.VMEM((n, 16, d.vec_lanes), F32),
         pltpu.VMEM((n, 16, d.vec_lanes), F32),
         pltpu.VMEM((16, d.vec_lanes), F32),
@@ -1036,29 +1071,24 @@
 
 
 def finalize(d, args):
-    rows, share, cols = d.rows, d.share, d.cols
-
-    def kernel(out_p, grad_p, g_qkv, g_out, g_up, g_down, g_vec, *outs):
-        output, input_grad, q, k, v, o, up, down = outs[:8]
-        output[...] = out_p[:rows, :]
-        input_grad[...] = grad_p[:rows, :]
-        for i, ref in enumerate((q, k, v)):
-            ref[...] = g_qkv[:, i * cols : (i + 1) * cols]
-        o[...] = g_out[...]
-        up[...] = g_up[:, : d.hidden]
-        down[...] = g_down[:, : d.hidden]
-        for i, ref in enumerate(outs[8:]):
+    names = len(args) - 1
+    f32 = partial(shape, dtype=F32)
+    outs = [shape(d.rows, d.width), f32(d.rows, d.width)] + [f32(*a.shape) for a in args[2:-1]]
+    vectors = [f32(d.share)] * 8 + [f32(d.up_share)]
+
+    def kernel(*refs):
+        ins, g_vec, results = refs[:names], refs[names], refs[names + 1 :]
+        for src, dst in zip(ins, results):
+            dst[...] = src[: dst.shape[0], :]
+        for i, ref in enumerate(results[names:]):
             m = ref.shape[0]
             ref[...] = jnp.reshape(g_vec[i : i + 1, :m], (m,))
 
-    f32 = partial(shape, dtype=F32)
-    outs = [shape(rows, d.width), f32(rows, d.width)] + [f32(share, cols)] * 3
-    outs += [f32(share, cols), f32(share, d.hidden), f32(share, d.hidden)] + [f32(share)] * 8 + [f32(d.up_share)]
     return pl.pallas_call(
         kernel,
-        out_shape=outs,
+        out_shape=outs + vectors,
         in_specs=[VM] * len(args),
-        out_specs=[VM] * len(outs),
+        out_specs=[VM] * (names + 9),
         compiler_params=pltpu.CompilerParams(vmem_limit_bytes=VMEM_BYTES),
         name="finalize",
     )(*args)

time: 228 us -> 214 us (0.939)
  Pallas kernels: 227 us -> 213 us
    pallas_call x1, Pallas kernels: 93.8 us -> 79.6 us  [backward(): pl.pallas_call(kernel, out_shape=outs, in_specs=[VM] * 7 + [ANY] * 10, ou...]
where the time goes in v3:
time: 214 us
  Pallas kernels  213 us (100%)
    pallas_call x1, Pallas kernels, forward(): pl.pallas_call(kernel, out_shape=outs + kept, in_specs=[VM] * len(args),...  130 us
    pallas_call x1, Pallas kernels, backward(): pl.pallas_call(kernel, out_shape=outs, in_specs=[VM] * 7 + [ANY] * 10, ou...  79.6 us

profile of v3, /device:TPU:0, one launch (start us, length us, event | category | flops | bytes accessed | tf_op | source)
XLA Modules:
  0.0 213.8 jit_solution(2301496616882112678)
XLA Ops:
  0.7 129.6 %forward.1 = (f32[16,1152]{1,0:T(8,128)}, f32[192,1152]{1,0:T(8,128)}, bf16[192,1152]{1,0:T(8,128)(2,1)}, f32[192,1152]{1,0:T(8,128)}, f32[8,1152]{1,0:T(8,128)}...) custom-call(bf16[184,1152]{1,0:T(8,128)(2,1)} %bitcast.8, ...), custom_call_target="tpu_custom_call" | custom-call | tf_op jit(solution)/shard_map/forward/pallas_call | solution.py:721
  130.2 79.6 %backward.1 = (bf16[192,1152]{1,0:T(8,128)(2,1)}, f32[192,1152]{1,0:T(8,128)}, f32[144,288]{1,0:T(8,128)}, f32[144,288]{1,0:T(8,128)}, f32[144,288]{1,0:T(8,128)...) custom-call(bf16[184,1152]{1,0:T(8,128)(2,1)} %bitcast.9, ...), custom_call_target="tpu_custom_call" | custom-call | tf_op jit(solution)/shard_map/backward/pallas_call | solution.py:1062
  209.8 3.8 %finalize.1 = (bf16[184,1152]{1,0:T(8,128)(2,1)}, f32[184,1152]{1,0:T(8,128)}, f32[144,288]{1,0:T(8,128)}, f32[144,288]{1,0:T(8,128)}, f32[144,288]{1,0:T(8,128)...) custom-call(bf16[192,1152]{1,0:T(8,128)(2,1)} %get-tuple-element.73., ...), custom_call_target="tpu_custom_call" | custom-call | tf_op jit(solution)/shard_map/finalize/pallas_call | solution.py:1087

commit v4 on v3

--- a/solution.py
+++ b/solution.py
@@ -183,7 +183,8 @@
         p = self.p
         block = self.dst.at[p.z]
         for k in range(1, p.line):
-            remote(block, block, self.sent.at[k], self.recv.at[p.z], p.along(k)).start()
+            step = jnp.where(p.z < p.line // 2, p.line - k, k)
+            remote(block, block, self.sent.at[k], self.recv.at[p.z], p.along(step)).start()
 
     def finish(self):
         p = self.p
@@ -408,12 +409,12 @@
         take = lambda m: [refs.pop(0) for _ in range(m)]
         tok, cot_in, mask, wq, wk, wv, wo, wu, wd = take(9)
         vecs = take(9)
-        vec, hidden, mixed_rows, grad_second, bias_part = take(5)
-        kept_out = take(10)
-        kept = take(10)
-        qh, kh, vh, mix, probs, first, wqkv, out_t, grads, o_part = kept
+        (grad_second,) = take(1)
+        kept_out = take(14)
+        kept = take(14)
+        qh, kh, vh, mix, probs, first, wqkv, out_t, grads, o_part, vec, hidden, mixed_rows, bias_part = kept
         tokbuf, w_st, o_mid, o_pack, u_st, d_st, v_st, v_all = take(8)
-        mixbuf, second, cot, up, down, act, pre_grad, part, inbox, upb, total = take(11)
+        mixbuf, second, cot, up, down, act, pre_grad, part, inbox, upb, total, grad_act = take(12)
         place = Place(n, t)
         place.greet()
         z = place.z
@@ -467,6 +468,7 @@
         bias_part[...] = jnp.zeros_like(bias_part)
         g_vec.forward()
         g_vec.finish()
+        vec[8:, :] = jnp.zeros((8, D), F32)
         for i in range(8):
             vec[i : i + 1, :] = jnp.concatenate([v_all[j, i : i + 1, : d.share] for j in range(n)], axis=1)
         upb[...] = jnp.zeros_like(upb)
@@ -539,7 +541,7 @@
                 g_out.forward()
             both_sides(place, s, norm_and_project)
         g_up.forward()
-        keep(0, 1, 2, 5, 6)
+        keep(0, 1, 2, 5, 6, 10)
 
         count = jnp.sum(mask[...].astype(F32), axis=1, keepdims=True)
         valid = valid_keys(d, count)
@@ -579,12 +581,23 @@
 
         def block(i, carry):
             r = order(i)
-            l_mix(r).finish()
-
-            @pl.when(jnp.logical_and(i == 2, jnp.logical_not(at_end)))
+
+            @pl.when(jnp.logical_and(i == 1, jnp.logical_not(at_end)))
             def _():
                 for slot in range(1, t - 1):
                     l_cot.relay(slot)
+
+            @pl.when(at_end)
+            def _():
+                l_cot.relay(r)
+
+            @pl.when(i == 0)
+            def _():
+                g_down.forward()
+                g_down.finish()
+
+            grad_act[...] = dot(cot[r], down[...], NN)
+            l_mix(r).finish()
 
             rows = jnp.concatenate(
                 [
@@ -608,17 +621,7 @@
             pre = dot(second[r], up[...], NN) + upb[0:1, :]
             value, slope = gelu_both(pre)
             act[r] = value.astype(BF16)
-
-            @pl.when(at_end)
-            def _():
-                l_cot.relay(r)
-
-            @pl.when(i == 0)
-            def _():
-                g_down.forward()
-                g_down.finish()
-
-            grad = dot(cot[r], down[...], NN) * slope
+            grad = grad_act[...] * slope
             bias_part[0:1, :] += jnp.sum(grad, axis=0, keepdims=True)
             pre_grad[r] = grad.astype(BF16)
             part[r] = dot(pre_grad[r], up[...], NT).astype(BF16)
@@ -662,24 +665,18 @@
                     chain.hop(h, order(i - h))
         for item in work:
             item()
-        keep(8, 9)
+        keep(8, 9, 11, 12, 13)
         for (lo, m), chain in zip(split, chains):
             chain.finish(grad_second, pl.ds(lo, m))
         if R > d.sent_rows:
             grad_second[d.sent_rows :, :] = jnp.zeros((R - d.sent_rows, D), F32)
         for op in (l_tok, l_cot):
             op.finish()
-        for i in range(10):
+        for i in range(14):
             pltpu.make_async_copy(kept[i], kept_out[i], kept_sems.at[i]).wait()
 
     heads = (d.heads, d.seq, HD)
-    outs = [
-        shape(16, D, dtype=F32),
-        shape(R, D, dtype=F32),
-        shape(R, D),
-        shape(R, D, dtype=F32),
-        shape(8, HP, dtype=F32),
-    ]
+    outs = [shape(R, D, dtype=F32)]
     kept = [
         shape(*heads),
         shape(*heads),
@@ -691,6 +688,10 @@
         shape(D, D),
         shape(2, D, HP),
         shape(t, R, D),
+        shape(16, D, dtype=F32),
+        shape(R, D, dtype=F32),
+        shape(R, D),
+        shape(8, HP, dtype=F32),
     ]
     scratch = [pltpu.VMEM(a.shape, a.dtype) for a in kept]
     scratch += [
@@ -713,11 +714,12 @@
         pltpu.VMEM((t + 1, R, D), BF16),
         pltpu.VMEM((8, HP), F32),
         pltpu.VMEM((R, D), F32),
+        pltpu.VMEM((R, HP), F32),
     ]
     for _ in range(5):
         scratch += DpGather.sems(chips)
     scratch += LineGather.sems(t) + DirectGather.sems(t) + LineGather.sems(t) + DirectGather.sems(t, (t,))
-    scratch += LineChain.sems(t) * 2 + [DMA((10,))]
+    scratch += LineChain.sems(t) * 2 + [DMA((14,))]
     return pl.pallas_call(
         kernel,
         out_shape=outs + kept,
@@ -784,11 +786,11 @@
     def kernel(*refs):
         refs = list(refs)
         take = lambda m: [refs.pop(0) for _ in range(m)]
-        tok, cot, hidden, grad_second, vec, mixed_rows, bias_part = take(7)
-        far = take(10)
+        tok, cot = take(2)
+        far = take(15)
         output, input_grad, g_q, g_k, g_v, g_out, g_up, g_down, g_vec = take(9)
-        near = take(10)
-        qh, kh, vh, mix, probs, first, wqkv, out_t, grads_mlp, p_part = near
+        near = take(15)
+        grad_second, qh, kh, vh, mix, probs, first, wqkv, out_t, grads_mlp, p_part, vec, hidden, mixed_rows, bias_part = near
         tok_p, cot_p, gh, low, send, got, dq, dk, dv, q_sum, grads = take(11)
         o_part, w_part, f_part, f_inbox, p_inbox, f_sum, acc = take(7)
         o_mid, o_got, v_send, v_got, v_mid, v_line = take(6)
@@ -811,8 +813,8 @@
         p_chains = [LineChain(place, view(p_part, *h), view(p_inbox, *h), take(2)) for h in split]
         exchange = LineExchange(place, o_mid, o_got, take(3))
         x_sent, x_recv, v_sent, v_recv, v_sent_line, v_recv_line, far_sems = take(7)
-        load = lambda i: pltpu.make_async_copy(far[i], near[i], far_sems.at[i])
-        for i in (9, 8, 7, 4, 0, 1, 2, 3, 6, 5):
+        load = lambda i: pltpu.make_async_copy(far[i + 1], near[i + 1], far_sems.at[i + 1])
+        for i in (9, 11, -1, 10, 8, 7, 12, 4, 0, 1, 2, 3, 6, 5, 13):
             load(i).start()
         place.meet()
         load(9).wait()
@@ -846,6 +848,8 @@
             add_row(4, total)
             add_row(7, cots)
 
+        for i in (11, -1, 10):
+            load(i).wait()
         chunks(d, norm_two)
         load(7).wait()
         mixed_grad = dot(low[...], out_t[...], NN).astype(BF16)
@@ -864,6 +868,7 @@
         p_chains[0].launch_left(t - 2)
         sum_up.move()
         third = D // 3
+        load(12).wait()
         for i in range(3):
             o_part[i * third : (i + 1) * third, :] = dot(
                 low[:, i * third : (i + 1) * third], mixed_rows[...], TN
@@ -905,8 +910,8 @@
                 sum_out.move()
                 for chain in p_chains:
                     chain.tick_far(1)
-        load(6).wait()
-        load(5).wait()
+        for i in (6, 5, 13):
+            load(i).wait()
 
         def part_block(i):
             slot = jnp.where(z < t // 2, t - 1 - i, i)
@@ -1028,7 +1033,7 @@
         shape(16, d.vec_lanes, dtype=F32),
     ]
     heads = (d.heads, d.seq, HD)
-    scratch = [pltpu.VMEM(a.shape, a.dtype) for a in args[7:]]
+    scratch = [pltpu.VMEM(a.shape, a.dtype) for a in args[2:]]
     scratch += [
         pltpu.VMEM((R, D), BF16),
         pltpu.VMEM((R, D), BF16),
@@ -1058,11 +1063,11 @@
     for width in (HP, HP, D, wide):
         scratch += [pltpu.VMEM((chips, share, width), BF16), pltpu.VMEM((chips - 1, share, width), BF16)]
     scratch += DpAdd.sems(chips) * 4 + LineChain.sems(t) * 4 + LineExchange.sems(t)
-    scratch += [DMA((t,)), DMA((t,)), DMA((n,)), DMA((n,)), DMA((t,)), DMA((t,)), DMA((10,))]
+    scratch += [DMA((t,)), DMA((t,)), DMA((n,)), DMA((n,)), DMA((t,)), DMA((t,)), DMA((15,))]
     return pl.pallas_call(
         kernel,
         out_shape=outs,
-        in_specs=[VM] * 7 + [ANY] * 10,
+        in_specs=[VM] * 2 + [ANY] * 15,
         out_specs=[VM] * len(outs),
         scratch_shapes=scratch,
         compiler_params=params(1),
@@ -1120,13 +1125,13 @@
     cols, hidden_cols = query_weight.shape[1], up_weight.shape[1]
     d = Dims(sizes, rows, width, share, cols, hidden_cols, up_share)
     small = [first_gain, first_shift, query_bias, value_bias, out_bias, second_gain, second_shift, down_bias]
-    vec, hidden, mixed_rows, grad_second, bias_part, *kept = forward(
+    kept = forward(
         d,
         [tokens[0], cotangent[0], key_mask, query_weight, key_weight, value_weight, out_weight.T, up_weight, down_weight.T]
         + small
         + [up_bias],
     )
-    parts = backward(d, [tokens[0], cotangent[0], hidden, grad_second, vec, mixed_rows, bias_part, *kept])
+    parts = backward(d, [tokens[0], cotangent[0], *kept])
     outs = finalize(d, parts)
     vectors = outs[8:]
     return (outs[0][None], outs[1][None], *outs[2:5], outs[5].T, outs[6], outs[7].T, *vectors[:7], vectors[8], vectors[7])

time: 214 us -> 210 us (0.981)
  Pallas kernels: 213 us -> 209 us
    pallas_call x1, Pallas kernels: 130 us -> 126 us  [forward(): pl.pallas_call(kernel, out_shape=outs + kept, in_specs=[VM] * len(args),...]
where the time goes in v4:
time: 210 us; the launch traced here: 209 us
  Pallas kernels  209 us (100%)
    pallas_call x1, Pallas kernels, forward(): pl.pallas_call(kernel, out_shape=outs + kept, in_specs=[VM] * len(args),...  126 us
    pallas_call x1, Pallas kernels, backward(): pl.pallas_call(kernel, out_shape=outs, in_specs=[VM] * 2 + [ANY] * 15, ou...  78.7 us

profile of v4, /device:TPU:0, one launch (start us, length us, event | category | flops | bytes accessed | tf_op | source)
XLA Modules:
  0.0 209.4 jit_solution(924324711121358576)
XLA Ops:
  0.7 126.1 %forward.1 = (f32[192,1152]{1,0:T(8,128)}, bf16[4,768,72]{2,1,0:T(8,128)(2,1)}, bf16[4,768,72]{2,1,0:T(8,128)(2,1)}, bf16[4,768,72]{2,1,0:T(8,128)(2,1)}, bf16[4...) custom-call(bf16[184,1152]{1,0:T(8,128)(2,1)} %bitcast.8, ...), custom_call_target="tpu_custom_call" | custom-call | tf_op jit(solution)/shard_map/forward/pallas_call | solution.py:723
  126.7 78.7 %backward.1 = (bf16[192,1152]{1,0:T(8,128)(2,1)}, f32[192,1152]{1,0:T(8,128)}, f32[144,288]{1,0:T(8,128)}, f32[144,288]{1,0:T(8,128)}, f32[144,288]{1,0:T(8,128)...) custom-call(bf16[184,1152]{1,0:T(8,128)(2,1)} %bitcast.9, ...), custom_call_target="tpu_custom_call" | custom-call | tf_op jit(solution)/shard_map/backward/pallas_call | solution.py:1067
  205.4 3.8 %finalize.1 = (bf16[184,1152]{1,0:T(8,128)(2,1)}, f32[184,1152]{1,0:T(8,128)}, f32[144,288]{1,0:T(8,128)}, f32[144,288]{1,0:T(8,128)}, f32[144,288]{1,0:T(8,128)...) custom-call(bf16[192,1152]{1,0:T(8,128)(2,1)} %get-tuple-element.73., ...), custom_call_target="tpu_custom_call" | custom-call | tf_op jit(solution)/shard_map/finalize/pallas_call | solution.py:1092

commit v5 on v4

--- a/solution.py
+++ b/solution.py
@@ -451,10 +451,10 @@
             v_st[i : i + 1, :m] = jnp.reshape(v[...].astype(F32), (1, m))
         o_mid[z] = jnp.concatenate([wo[i * d.fold : (i + 1) * d.fold, :] for i in range(d.folds)], axis=1)
         place.meet()
-        l_out.start()
         g_vec.start()
         g_qkv.start()
         l_tok.start()
+        l_out.start()
         at_end = jnp.logical_or(z == 0, z == t - 1)
 
         @pl.when(at_end)
@@ -463,6 +463,7 @@
 
         u_st[...] = jnp.zeros_like(u_st)
         u_st[:, : d.hidden] = wu[...]
+        g_up.start()
         d_st[...] = jnp.zeros_like(d_st)
         d_st[:, : d.hidden] = wd[...]
         bias_part[...] = jnp.zeros_like(bias_part)
@@ -501,16 +502,15 @@
                     ref[j, at, :] = y[:, start : start + HD]
 
         norm_block(z)
+        l_tok.step(1)
         l_out.finish()
         for i in range(d.folds):
             o_pack[i * d.fold : (i + 1) * d.fold, :] = jnp.concatenate(
                 [o_mid[j, :, i * d.cols : (i + 1) * d.cols] for j in range(t)], axis=1
             )
         g_out.start()
-        l_tok.step(1)
+        g_down.start()
         g_qkv.forward()
-        g_up.start()
-        g_down.start()
         both_sides(place, 1, norm_block)
         g_qkv.finish()
         project_block(z)
@@ -538,9 +538,9 @@
                     l_cot.start()
 
             if s == 2:
-                g_out.forward()
+                g_up.forward()
             both_sides(place, s, norm_and_project)
-        g_up.forward()
+        g_out.forward()
         keep(0, 1, 2, 5, 6, 10)
 
         count = jnp.sum(mask[...].astype(F32), axis=1, keepdims=True)
@@ -818,9 +818,8 @@
             load(i).start()
         place.meet()
         load(9).wait()
-        for chain in p_chains:
-            chain.launch_right(t - 1)
-            chain.launch_left(0)
+        p_chains[0].launch_right(t - 1)
+        p_chains[0].launch_left(0)
         load(8).wait()
         sum_up.start()
         sum_down.start()
@@ -860,6 +859,9 @@
             to = place.along(k)
             remote(send.at[to[1]], got.at[z], x_sent.at[k], x_recv.at[z], to).start()
         got[z] = send[z]
+        for chain in p_chains[1:]:
+            chain.launch_right(t - 1)
+            chain.launch_left(0)
         for i in range(t - 2, 1, -1):
             for chain in p_chains:
                 chain.launch_right(i)
@@ -912,6 +914,9 @@
                     chain.tick_far(1)
         for i in (6, 5, 13):
             load(i).wait()
+        for i in range(2, t - 1):
+            for chain in p_chains:
+                chain.tick_far(i)
 
         def part_block(i):
             slot = jnp.where(z < t // 2, t - 1 - i, i)
@@ -935,9 +940,6 @@
         for chain in p_chains[1:]:
             chain.launch_right(1)
             chain.launch_left(t - 2)
-        for i in range(2, t - 1):
-            for chain in p_chains:
-                chain.tick_far(i)
 
         def weight_block(i):
             value = first[:, :, i * third : (i + 1) * third].reshape(d.seq, third)

time: 210 us -> 209 us (level)
  no operation moved by 1% of the time
where the time goes in v5:
time: 209 us
  Pallas kernels  208 us (100%)
    pallas_call x1, Pallas kernels, forward(): pl.pallas_call(kernel, out_shape=outs + kept, in_specs=[VM] * len(args),...  126 us
    pallas_call x1, Pallas kernels, backward(): pl.pallas_call(kernel, out_shape=outs, in_specs=[VM] * 2 + [ANY] * 15, ou...  77.8 us

profile of v5, /device:TPU:0, one launch (start us, length us, event | category | flops | bytes accessed | tf_op | source)
XLA Modules:
  0.0 208.7 jit_solution(17433385067146548541)
XLA Ops:
  0.7 126.1 %forward.1 = (f32[192,1152]{1,0:T(8,128)}, bf16[4,768,72]{2,1,0:T(8,128)(2,1)}, bf16[4,768,72]{2,1,0:T(8,128)(2,1)}, bf16[4,768,72]{2,1,0:T(8,128)(2,1)}, bf16[4...) custom-call(bf16[184,1152]{1,0:T(8,128)(2,1)} %bitcast.8, ...), custom_call_target="tpu_custom_call" | custom-call | tf_op jit(solution)/shard_map/forward/pallas_call | solution.py:723
  126.8 77.8 %backward.1 = (bf16[192,1152]{1,0:T(8,128)(2,1)}, f32[192,1152]{1,0:T(8,128)}, f32[144,288]{1,0:T(8,128)}, f32[144,288]{1,0:T(8,128)}, f32[144,288]{1,0:T(8,128)...) custom-call(bf16[184,1152]{1,0:T(8,128)(2,1)} %bitcast.9, ...), custom_call_target="tpu_custom_call" | custom-call | tf_op jit(solution)/shard_map/backward/pallas_call | solution.py:1069
  204.7 3.8 %finalize.1 = (bf16[184,1152]{1,0:T(8,128)(2,1)}, f32[184,1152]{1,0:T(8,128)}, f32[144,288]{1,0:T(8,128)}, f32[144,288]{1,0:T(8,128)}, f32[144,288]{1,0:T(8,128)...) custom-call(bf16[192,1152]{1,0:T(8,128)(2,1)} %get-tuple-element.73., ...), custom_call_target="tpu_custom_call" | custom-call | tf_op jit(solution)/shard_map/finalize/pallas_call | solution.py:1094

commit v6 on v5

--- a/solution.py
+++ b/solution.py
@@ -1068,7 +1068,7 @@
     scratch += [DMA((t,)), DMA((t,)), DMA((n,)), DMA((n,)), DMA((t,)), DMA((t,)), DMA((15,))]
     return pl.pallas_call(
         kernel,
-        out_shape=outs,
+        out_shape=[pltpu.VMEM(a.shape, a.dtype) for a in outs],
         in_specs=[VM] * 2 + [ANY] * 15,
         out_specs=[VM] * len(outs),
         scratch_shapes=scratch,
@@ -1134,7 +1134,7 @@
         + [up_bias],
     )
     parts = backward(d, [tokens[0], cotangent[0], *kept])
-    outs = finalize(d, parts)
+    outs = finalize(d, [pltpu.with_memory_space_constraint(p, pltpu.VMEM) for p in parts])
     vectors = outs[8:]
     return (outs[0][None], outs[1][None], *outs[2:5], outs[5].T, outs[6], outs[7].T, *vectors[:7], vectors[8], vectors[7])
 

time: 209 us -> 205 us (0.981)
  Pallas kernels: 208 us -> 204 us
where the time goes in v6:
time: 205 us
  Pallas kernels  204 us (100%)
    pallas_call x1, Pallas kernels, forward(): pl.pallas_call(kernel, out_shape=outs + kept, in_specs=[VM] * len(args),...  126 us
    pallas_call x1, Pallas kernels, backward(): pl.pallas_call(kernel, out_shape=[pltpu.VMEM(a.shape, a.dtype) for a in o...  76 us

profile of v6, /device:TPU:0, one launch (start us, length us, event | category | flops | bytes accessed | tf_op | source)
XLA Modules:
  0.0 205.0 jit_solution(6754381088427357765)
XLA Ops:
  0.7 126.1 %forward.1 = (f32[192,1152]{1,0:T(8,128)}, bf16[4,768,72]{2,1,0:T(8,128)(2,1)}, bf16[4,768,72]{2,1,0:T(8,128)(2,1)}, bf16[4,768,72]{2,1,0:T(8,128)(2,1)}, bf16[4...) custom-call(bf16[184,1152]{1,0:T(8,128)(2,1)} %bitcast.8, ...), custom_call_target="tpu_custom_call" | custom-call | tf_op jit(solution)/shard_map/forward/pallas_call | solution.py:723
  126.7 76.0 %backward.1 = (bf16[192,1152]{1,0:T(8,128)(2,1)S(1)}, f32[192,1152]{1,0:T(8,128)S(1)}, f32[144,288]{1,0:T(8,128)S(1)}, f32[144,288]{1,0:T(8,128)S(1)}, f32[144,2...) custom-call(bf16[184,1152]{1,0:T(8,128)(2,1)} %bitcast.9, ...), custom_call_target="tpu_custom_call" | custom-call | tf_op jit(solution)/shard_map/backward/pallas_call | solution.py:1069
  202.8 2.0 finalize.1
